TPU v7x, 32 devices: a whole 2x2x4 slice. The times are simulated.
32 devices in a mesh: dp: 8 (over z, y), ctx: 4 (over x, core).
Axes of the slice: x: 2, y: 2, z: 4, core: 2. Of those that a mesh axis runs over, the one named last changes fastest.
Arguments:
- tokens: bfloat16 [8, 1024, 4096], P('dp', 'ctx'), may hold values from -7 to 7
- block_order: int32 [8, 8], P('dp', 'ctx'), may hold values from 0 to 7, as said below
- doc_ids: int32 [8, 1024], P('dp', 'ctx'), may hold values from 0 to 1, as said below
- w_qkv: bfloat16 [4096, 768], P('dp'), as said below
- grad_out: bfloat16 [8, 1024, 512], P('dp', 'ctx'), may hold values from -6 to 6
Outputs:
- attended: bfloat16 [8, 1024, 512], P('dp', 'ctx')
- grad_tokens: bfloat16 [8, 1024, 4096], P('dp', 'ctx')
- grad_w: float32 [4096, 768], P(('dp', 'ctx'))
Inputs may be any that keep to these rules, and one draw needn't show every extreme that they name: `block_order`: each row holds every block number of its sequence once; stored blocks 2 r and 2 r + 1 hold numbers that sum to 7. `doc_ids`: taken in order of sequence position, a sequence's document numbers start at 0, never fall and rise by at most one; every sequence reaches the largest number. `w_qkv`: entries lie within 4 / sqrt(4096) of zero.
All inputs are finite; a program needn't handle non-finite values.
Results may differ from a plain program's by a relative error of at most 0.02.
Values may be sent and summed in bfloat16 or wider, within the bound.
No kernel may reach another device: no remote copies, remote signals or barrier semaphores. Data moves between devices by JAX's collectives and lax.ppermute only.
A program may use at most 128 MiB of HBM per device.

v0:
```python
import math
from functools import partial

import jax
import jax.numpy as jnp
from jax import lax
from jax.experimental import pallas as pl
from jax.experimental.pallas import tpu as pltpu
from jax.sharding import PartitionSpec as P


HQ = 4
HD = 128
BLOCK = 128
WQ = HQ * HD
ROPE_BASE = 500000.0
NEG_FILL = -1e30
BF16 = jnp.bfloat16
F32 = jnp.float32
VMEM_GRANT = 16 << 20


def rope_tables(positions):
    half = HD // 2
    inverse = 1.0 / ROPE_BASE ** (jnp.arange(half, dtype=F32) * (2.0 / HD))
    angles = positions.astype(F32)[..., None] * inverse
    return (jnp.cos(angles), jnp.sin(angles))


def rotate(values, cosine_table, sine_table):
    half = values.shape[-1] // 2
    leading = values[..., :half]
    trailing = values[..., half:]
    return jnp.concatenate(
        [
            leading * cosine_table - trailing * sine_table,
            trailing * cosine_table + leading * sine_table,
        ],
        axis=-1,
    )


def flip_bits(array, axis, size, index):
    bit = 1
    while bit < size:
        shape = array.shape
        split = array.reshape(shape[:axis] + (size // (2 * bit), 2, bit) + shape[axis + 1 :])
        array = jnp.where((index & bit) != 0, jnp.flip(split, axis + 1), split).reshape(shape)
        bit *= 2
    return array


def exchange(array, axis, size, offset):
    return lax.ppermute(array, axis, [(i, i ^ offset) for i in range(size)])


def block_kernel(dims, width, scatter, index_ref, in_ref, out_ref):
    n_core, n_x, n_y, n_z = dims
    row, col = index_ref[0], index_ref[1]
    for p in range(n_core * n_x * n_y * n_z):
        jz, rest = p % n_z, p // n_z
        jy, rest = rest % n_y, rest // n_y
        jx, jc = rest % n_x, rest // n_x
        place = (row ^ (jz * n_y + jy)) * (n_x * n_core) + (col ^ (jx * n_core + jc))
        dynamic = pl.ds(pl.multiple_of(place * width, width), width)
        static = pl.ds(p * width, width)
        if scatter:
            out_ref[:, dynamic] = in_ref[:, static]
        else:
            out_ref[:, static] = in_ref[:, dynamic]


def reorder(array, dims, row, col, scatter):
    n_core, n_x, n_y, n_z = dims
    width = array.shape[1] // (n_core * n_x * n_y * n_z)
    if width % 128 == 0:
        return pl.pallas_call(
            partial(block_kernel, dims, width, scatter),
            out_shape=jax.ShapeDtypeStruct(array.shape, array.dtype),
            grid_spec=pltpu.PrefetchScalarGridSpec(
                num_scalar_prefetch=1,
                grid=(1,),
                in_specs=[pl.BlockSpec(array.shape, lambda i, s: (0, 0))],
                out_specs=pl.BlockSpec(array.shape, lambda i, s: (0, 0)),
            ),
            cost_estimate=pl.CostEstimate(
                flops=0, bytes_accessed=4 * array.size, transcendentals=0
            ),
            name="scatter_columns" if scatter else "gather_columns",
        )(jnp.stack([row, col]).astype(jnp.int32), array)
    count = array.shape[0]
    rows, cols = n_y * n_z, n_x * n_core
    if scatter:
        split = array.reshape(count, n_core, n_x, n_y, n_z, width).transpose(0, 4, 3, 2, 1, 5)
    else:
        split = array
    split = split.reshape(count, rows, cols, width)
    split = flip_bits(flip_bits(split, 1, rows, row), 2, cols, col)
    if not scatter:
        split = split.reshape(count, n_z, n_y, n_x, n_core, width).transpose(0, 4, 3, 2, 1, 5)
    return split.reshape(array.shape)


def on_device(n_dp, n_ctx, tokens, block_order, doc_ids, w_qkv, grad_out):
    inputs = tokens[0]
    row_count, features = inputs.shape
    score_scale = 1.0 / math.sqrt(HD)
    n_core, n_x = 2, n_ctx // 2
    n_z = 4
    n_y = n_dp // n_z
    dims = (n_core, n_x, n_y, n_z)
    row, col = lax.axis_index("dp"), lax.axis_index("ctx")
    over_z = lambda a, o: exchange(a, "dp", n_dp, o * n_y)
    over_y = lambda a, o: exchange(a, "dp", n_dp, o)
    over_x = lambda a, o: exchange(a, "ctx", n_ctx, o * n_core)
    over_core = lambda a: exchange(a, "ctx", n_ctx, 1)
    near = lambda n: range(1, n)

    facts = jnp.concatenate([doc_ids[0], block_order[0]])
    facts_x = jnp.stack([facts] + [over_x(facts, o) for o in near(n_x)])
    facts_all = jnp.stack([facts_x, over_core(facts_x)]).reshape(n_ctx, -1)
    docs_all = facts_all[:, :row_count].reshape(-1)
    order_all = facts_all[:, row_count:]
    pos_all = (order_all[:, :, None] * BLOCK + jnp.arange(BLOCK, dtype=jnp.int32)).reshape(-1)
    docs_here, pos_here = docs_all[:row_count], pos_all[:row_count]

    shard = w_qkv.shape[0]
    piece = shard // n_ctx
    own = w_qkv.reshape(n_x * n_core, piece, -1)
    own = flip_bits(own, 0, n_ctx, col).reshape(n_x, n_core, piece, -1)

    def gather_yz(first):
        by_z = jnp.stack([first] + [over_z(first, o) for o in near(n_z)])
        rows = [by_z]
        for o in near(n_y):
            rows.append(jnp.concatenate([over_y(first, o)[None], over_y(by_z[1:], o)]))
        return jnp.stack(rows)

    kv_half = gather_yz(own[:, 0, :, WQ:])
    kv_half = jnp.moveaxis(kv_half, 2, 0)
    kv_half = jnp.stack([kv_half, over_core(kv_half)])
    w_kv = kv_half.reshape(features, 2 * HD)

    q_part = gather_yz(own[0, 0, :, :WQ])
    q_half = jnp.stack([q_part] + [over_x(q_part, o) for o in near(n_x)])
    q_full = jnp.stack([q_half, over_core(q_half)])
    w_q = q_full.reshape(features, WQ)

    near_inputs = reorder(inputs, dims, row, col, False)
    projected_kv = jnp.dot(near_inputs, w_kv, preferred_element_type=F32)
    cosine_table, sine_table = rope_tables(pos_here)
    key_here = rotate(projected_kv[:, :HD], cosine_table, sine_table).astype(BF16)
    value_here = projected_kv[:, HD:].astype(BF16)
    kv_here = jnp.concatenate([key_here, value_here], axis=1)
    kv_x = jnp.stack([kv_here] + [over_x(kv_here, o) for o in near(n_x)])
    kv_core = jnp.concatenate([over_core(kv_here)[None], over_core(kv_x[1:])])
    kv_all = jnp.concatenate([kv_x, kv_core]).reshape(-1, 2 * HD)
    keys, values = kv_all[:, :HD], kv_all[:, HD:]

    projected_q = jnp.dot(near_inputs, w_q, preferred_element_type=F32)
    queries = rotate(
        projected_q.reshape(row_count, HQ, HD),
        cosine_table[:, None, :],
        sine_table[:, None, :],
    ).astype(BF16)

    allowed = (docs_here[:, None] == docs_all[None, :]) & (pos_all[None, :] <= pos_here[:, None])
    allowed = allowed[:, None, :]
    scores = jnp.einsum("thd,nd->thn", queries, keys, preferred_element_type=F32) * score_scale
    row_max = jnp.max(jnp.where(allowed, scores, NEG_FILL), axis=-1)
    shifted = jnp.where(allowed, jnp.exp(scores - row_max[..., None]), 0.0)
    row_sum = jnp.sum(shifted, axis=-1)
    weighted = jnp.einsum("thn,nd->thd", shifted.astype(BF16), values, preferred_element_type=F32)
    attended = (weighted / row_sum[..., None]).astype(BF16)
    log_norm = row_max + jnp.log(row_sum)
    out_grad = grad_out[0].reshape(row_count, HQ, HD)
    row_dots = jnp.sum(out_grad.astype(F32) * attended.astype(F32), axis=-1)
    chances = jnp.where(allowed, jnp.exp(scores - log_norm[..., None]), 0.0)
    value_term = jnp.einsum(
        "thn,thd->nd", chances.astype(BF16), out_grad, preferred_element_type=F32
    )
    prob_grad = jnp.einsum("thd,nd->thn", out_grad, values, preferred_element_type=F32)
    score_grad = (chances * (prob_grad - row_dots[..., None])).astype(BF16)
    query_grad = (
        jnp.einsum("thn,nd->thd", score_grad, keys, preferred_element_type=F32) * score_scale
    )
    key_term = (
        jnp.einsum("thn,thd->nd", score_grad, queries, preferred_element_type=F32) * score_scale
    )
    kv_terms = jnp.concatenate([key_term, value_term], axis=1)
    kv_terms = kv_terms.reshape(n_core, n_x, row_count, 2 * HD)
    kv_sum = kv_terms[0] + over_core(kv_terms[1].astype(BF16)).astype(F32)
    kv_send = kv_sum[1:].astype(BF16)
    kv_mine = kv_sum[0]
    for o in near(n_x):
        kv_mine = kv_mine + over_x(kv_send[o - 1], o).astype(F32)

    q_grad = rotate(query_grad, cosine_table[:, None, :], -sine_table[:, None, :])
    q_grad = q_grad.reshape(row_count, WQ).astype(BF16)
    key_raw = rotate(kv_mine[:, :HD], cosine_table, -sine_table)
    kv_grad = jnp.concatenate([key_raw, kv_mine[:, HD:]], axis=1).astype(BF16)

    def weight_terms(columns, grad):
        return lax.dot_general(
            columns, grad, (((0,), (0,)), ((), ())), preferred_element_type=F32
        )

    half = features // 2

    def core_sum(grad):
        sent = over_core(weight_terms(near_inputs[:, half:], grad).astype(BF16))
        kept = weight_terms(near_inputs[:, :half], grad) + sent.astype(F32)
        return kept.reshape(n_x, n_y, n_z, piece, -1)

    def reduce_first(terms, over):
        total = terms[0]
        for o in near(terms.shape[0]):
            total = total + over(terms[o].astype(BF16), o).astype(F32)
        return total

    q_terms = core_sum(q_grad)
    q_terms = reduce_first(q_terms, over_x)
    q_terms = reduce_first(q_terms, over_y)
    q_terms = reduce_first(q_terms, over_z)

    kv_sums = core_sum(kv_grad)
    kv_sums = reduce_first(jnp.moveaxis(kv_sums, 0, 2), over_y)
    kv_sums = reduce_first(kv_sums, over_z)
    kv_sums = reduce_first(kv_sums, over_x)
    grad_w = jnp.concatenate([q_terms, kv_sums], axis=1)

    near_grad = (
        lax.dot_general(q_grad, w_q, (((1,), (1,)), ((), ())), preferred_element_type=F32)
        + lax.dot_general(kv_grad, w_kv, (((1,), (1,)), ((), ())), preferred_element_type=F32)
    ).astype(BF16)
    grad_inputs = reorder(near_grad, dims, row, col, True)
    return (attended.reshape(1, row_count, WQ), grad_inputs[None], grad_w)


def place_of(dims, p):
    n_core, n_x, n_y, n_z = dims
    jx, rest = p % n_x, p // n_x
    jy, rest = rest % n_y, rest // n_y
    jz, jc = rest % n_z, rest // n_z
    return (jz * n_y + jy), (jx * n_core + jc)


def vmem_call(body, out_shapes, operands, flops, blocks=None, scalars=None, scratch=()):
    blocks = blocks or {}
    count = len(operands)
    lead = 0 if scalars is None else 1

    def cut_body(*refs):
        refs = list(refs)
        for i, (start, size) in blocks.items():
            refs[lead + i] = refs[lead + i].at[pl.ds(start, size)]
        body(*refs)

    sizes = [math.prod(a.shape) * a.dtype.itemsize for a in operands]
    sizes += [math.prod(s.shape) * s.dtype.itemsize for s in out_shapes]
    whole = pl.BlockSpec(memory_space=pltpu.VMEM)
    return pl.pallas_call(
        cut_body,
        out_shape=out_shapes,
        in_specs=[pl.BlockSpec(memory_space=pltpu.SMEM)] * lead + [whole] * count,
        out_specs=[whole] * len(out_shapes),
        scratch_shapes=scratch,
        cost_estimate=pl.CostEstimate(flops=flops, bytes_accessed=sum(sizes), transcendentals=0),
        compiler_params=pltpu.CompilerParams(vmem_limit_bytes=VMEM_GRANT),
    )(*([] if scalars is None else [scalars]), *operands)


def shape_of(shape, dtype):
    return jax.ShapeDtypeStruct(shape, dtype)


def gather_tokens(inputs, dims, index):
    count, features = inputs.shape
    total = math.prod(dims)
    width = features // total
    n_k = dims[0] * dims[1]

    def body(index_ref, in_ref, near_ref, turned_ref, own_ref):
        row, col = index_ref[0], index_ref[1]
        for p in range(total):
            dr, dc = place_of(dims, p)
            place = (row ^ dr) * n_k + (col ^ dc)
            block = in_ref[:, pl.ds(pl.multiple_of(place * width, width), width)]
            near_ref[:, p * width : (p + 1) * width] = block
            turned_ref[p * width : (p + 1) * width, :] = block.astype(F32).T.astype(BF16)
        own_ref[...] = in_ref[:, pl.ds(pl.multiple_of(row * (n_k * width), width), n_k * width)]

    shapes = [
        shape_of((count, features), BF16),
        shape_of((features, count), BF16),
        shape_of((count, n_k * width), BF16),
    ]
    return vmem_call(body, shapes, [inputs], 0, scalars=index)


def turn(x, cos_table, sin_table):
    return x * cos_table + pltpu.roll(x, HD // 2, 1) * sin_table


def matmul(a, b, ca=1, cb=0):
    return lax.dot_general(a, b, (((ca,), (cb,)), ((), ())), preferred_element_type=F32)


def attention(first, late, near_inputs, late_places, width, kv_parts, tables, out_grad):
    count = first.shape[0]
    n_parts = len(kv_parts)
    n_keys = count * n_parts
    scale = 1.0 / math.sqrt(HD)
    n_late = len(late)

    def body(*refs):
        first_ref, near_ref = refs[:2]
        late_refs = refs[2 : 2 + n_late]
        rest = refs[2 + n_late :]
        kv_refs = rest[:n_parts]
        cos_ref, sin_ref, grad_ref = rest[n_parts : n_parts + 3]
        att_ref, qgrad_ref, far_ref, close_ref = rest[n_parts + 3 : n_parts + 7]
        kv_ref, kt_ref, vt_ref, bias_ref, acc_ref = rest[n_parts + 7 :]
        here = kv_refs[0][count:, :].astype(F32)
        within = lax.broadcasted_iota(jnp.int32, (1, count), 1) % BLOCK
        here_docs, here_pos = here[0:1], here[1:2] * BLOCK + within.astype(F32)
        within = lax.broadcasted_iota(jnp.int32, (count, 1), 0) % BLOCK
        for i, ref in enumerate(kv_refs):
            rows = slice(i * count, (i + 1) * count)
            kv_ref[rows, :] = ref[:count, :]
            there = ref[count:, :].astype(F32).T
            pos = there[:, 1:2] * BLOCK + within.astype(F32)
            allowed = (there[:, 0:1] == here_docs) & (pos <= here_pos)
            bias_ref[rows, :] = jnp.where(allowed, 0.0, NEG_FILL)
        kt_ref[...] = kv_ref[:, :HD].astype(F32).T.astype(BF16)
        vt_ref[...] = kv_ref[:, HD:].astype(F32).T.astype(BF16)
        cos_table, sin_table = cos_ref[...], sin_ref[...]
        queries = first_ref[:, :WQ]
        for ref, places in zip(late_refs, late_places):
            for i, p in enumerate(places):
                queries = queries + matmul(near_ref[:, p * width : (p + 1) * width], ref[i])
        keys, values = kv_ref[:, :HD], kv_ref[:, HD:]
        for h in range(HQ):
            cols = slice(h * HD, (h + 1) * HD)
            q = turn(queries[:, cols], cos_table, sin_table).astype(BF16)
            grad = grad_ref[:, cols]
            scores = matmul(keys, q, 1, 1) * scale + bias_ref[...]
            top = jnp.max(scores, axis=0, keepdims=True)
            shifted = jnp.exp(scores - top)
            total = jnp.sum(shifted, axis=0, keepdims=True)
            weighted = matmul(vt_ref[...], shifted.astype(BF16))
            att = (weighted / total).astype(BF16).astype(F32)
            att_ref[:, cols] = att.T.astype(BF16)
            dots = jnp.sum(grad.astype(F32).T * att, axis=0, keepdims=True)
            chances = shifted * (1.0 / total)
            value_term = matmul(chances.astype(BF16), grad)
            prob_grad = matmul(values, grad, 1, 1)
            score_grad = (chances * (prob_grad - dots)).astype(BF16)
            key_term = matmul(score_grad, q) * scale
            if h == 0:
                acc_ref[:, :HD] = key_term
                acc_ref[:, HD:] = value_term
            else:
                acc_ref[:, :HD] += key_term
                acc_ref[:, HD:] += value_term
            q_grad = matmul(kt_ref[...], score_grad).T * scale
            qgrad_ref[:, cols] = turn(q_grad, cos_table, -sin_table).astype(BF16)
        half = n_keys // 2
        close_ref[...] = acc_ref[:half, :]
        far_ref[...] = acc_ref[half:, :].astype(BF16)

    operands = [first, near_inputs, *late, *kv_parts, *tables, out_grad]
    shapes = [
        shape_of((count, WQ), BF16),
        shape_of((count, WQ), BF16),
        shape_of((n_keys // 2, 2 * HD), BF16),
        shape_of((n_keys // 2, 2 * HD), F32),
    ]
    return vmem_call(
        body,
        shapes,
        operands,
        14 * HQ * count * n_keys * HD,
        scratch=[
            pltpu.VMEM((n_keys, 2 * HD), BF16),
            pltpu.VMEM((HD, n_keys), BF16),
            pltpu.VMEM((HD, n_keys), BF16),
            pltpu.VMEM((n_keys, count), F32),
            pltpu.VMEM((n_keys, 2 * HD), F32),
        ],
    )


def near_device(n_dp, n_ctx, *args):
    return near_body(n_dp, n_ctx, *args)


def near_body(n_dp, n_ctx, tokens, block_order, doc_ids, w_qkv, grad_out):
    inputs = tokens[0]
    count, features = inputs.shape
    n_core, n_x, n_z = 2, 2, 4
    n_y = n_dp // n_z
    dims = (n_core, n_x, n_y, n_z)
    index = jnp.stack([lax.axis_index("dp"), lax.axis_index("ctx")]).astype(jnp.int32)
    index = lax.optimization_barrier(index)
    col = index[1]
    shard = w_qkv.shape[0]
    width = shard // n_ctx
    kv_w = 2 * HD

    over_z = lambda a, o: exchange(a, "dp", n_dp, o * n_y)
    over_y = lambda a: exchange(a, "dp", n_dp, 1)
    over_x = lambda a: exchange(a, "ctx", n_ctx, n_core)
    over_core = lambda a: exchange(a, "ctx", n_ctx, 1)
    spot = lambda jc, jz, jy, jx: ((jc * n_z + jz) * n_y + jy) * n_x + jx
    cut = lambda p: slice(p * width, (p + 1) * width)

    own_rows = lax.dynamic_slice_in_dim(w_qkv, col * width, width, 0)
    other_rows = lax.dynamic_slice_in_dim(w_qkv, (col ^ n_core) * width, width, 0)
    piece = jnp.concatenate([own_rows, other_rows[:, WQ:]], axis=1)
    by_z = {o: over_z(piece, o) for o in (1, 2, 3)}
    by_y = {0: over_y(piece)}
    for o in (1, 2, 3):
        by_y[o] = over_y(by_z[o])
    main = {(0, 1): by_y[0]}
    for o in (1, 2, 3):
        main[(o, 0)] = by_z[o]
        main[(o, 1)] = by_y[o]
    groups = [[(0, 1), (1, 0)], [(1, 1), (2, 0)], [(2, 1), (3, 0)], [(3, 1)]]
    side = [over_x(jnp.stack([main[k][:, :WQ] for k in group])) for group in groups]
    mains = [main, {k: over_core(a) for k, a in main.items()}]
    sides = [side, [over_core(a) for a in side]]

    near_inputs, turned, own_inputs = gather_tokens(inputs, dims, index)

    positions = (
        block_order[0][:, None] * BLOCK + jnp.arange(BLOCK, dtype=jnp.int32)
    ).reshape(count)
    cosine_table, sine_table = rope_tables(positions)
    cos_table = jnp.concatenate([cosine_table, cosine_table], axis=1)
    sin_table = jnp.concatenate([-sine_table, sine_table], axis=1)
    fact_rows = jnp.concatenate(
        [
            doc_ids.astype(BF16),
            jnp.repeat(block_order[0], BLOCK)[None].astype(BF16),
            jnp.zeros((14, count), BF16),
        ]
    )

    def project(start, keys, side_ids, last):
        operands, plan = [near_inputs], []
        for jc in range(n_core):
            for jz, jy in keys:
                plan.append(("main", jc, jz, jy, len(operands)))
                operands.append(mains[jc][(jz, jy)])
            for i in side_ids:
                plan.append(("side", jc, i, None, len(operands)))
                operands.append(sides[jc][i])
        n_in = len(operands)
        if start is None:
            operands += [own_inputs, w_qkv]
        else:
            operands += [start]
        if last:
            operands += [cos_table, sin_table, fact_rows]

        def body(*refs):
            near_ref = refs[0]
            if start is None:
                total = matmul(refs[n_in][...], refs[n_in + 1][...])
            else:
                total = refs[n_in][...]
            q_sum, kv_sum = total[:, :WQ], total[:, WQ:]
            for kind, jc, a, b, at in plan:
                ref = refs[at]
                if kind == "main":
                    part = matmul(near_ref[:, cut(spot(jc, a, b, 0))], ref[:, : WQ + kv_w])
                    q_sum = q_sum + part[:, :WQ]
                    kv_sum = kv_sum + part[:, WQ:]
                    kv_sum = kv_sum + matmul(
                        near_ref[:, cut(spot(jc, a, b, 1))], ref[:, WQ + kv_w :]
                    )
                else:
                    for i, (jz, jy) in enumerate(groups[a]):
                        q_sum = q_sum + matmul(near_ref[:, cut(spot(jc, jz, jy, 1))], ref[i])
            if last:
                cos_ref, sin_ref, fact_ref, out_ref, kv_ref = refs[-5:]
                out_ref[...] = q_sum
                kv_ref[:count, :HD] = turn(kv_sum[:, :HD], cos_ref[...], sin_ref[...]).astype(BF16)
                kv_ref[:count, HD:] = kv_sum[:, HD:].astype(BF16)
                kv_ref[count:, :] = fact_ref[...]
            else:
                refs[-1][:, :WQ] = q_sum
                refs[-1][:, WQ:] = kv_sum

        if last:
            shapes = [shape_of((count, WQ), F32), shape_of((count + 16, kv_w), BF16)]
        else:
            shapes = [shape_of((count, WQ + kv_w), F32)]
        flops = 2 * count * width * (WQ + 2 * kv_w) * len(plan)
        return vmem_call(body, shapes, operands, flops)

    (part,) = project(None, [(0, 1), (1, 0), (1, 1), (2, 0), (2, 1), (3, 0)], [0, 1], False)
    q_part, kv_here = project(part, [(3, 1)], [], True)

    kv_x = over_x(kv_here)
    kv_parts = [kv_here, kv_x, over_core(kv_here), over_core(kv_x)]
    late = [sides[jc][i] for jc in range(n_core) for i in (2, 3)]
    late_places = [
        [spot(jc, jz, jy, 1) for jz, jy in groups[i]] for jc in range(n_core) for i in (2, 3)
    ]
    attended, q_grad, kv_far, kv_close = attention(
        q_part,
        late,
        near_inputs,
        late_places,
        width,
        kv_parts,
        (cos_table, sin_table),
        grad_out[0],
    )

    kv_got = over_core(kv_far)

    def mid_body(close_ref, got_ref, out_ref):
        out_ref[...] = (close_ref[...] + got_ref[...].astype(F32)).astype(BF16)

    (kv_send,) = vmem_call(
        mid_body,
        [shape_of((count, kv_w), BF16)],
        [kv_close, kv_got],
        0,
        blocks={0: (count, count), 1: (count, count)},
    )
    kv_last = over_x(kv_send)

    def kv_body(close_ref, got_ref, last_ref, cos_ref, sin_ref, out_ref):
        total = close_ref[...] + got_ref[...].astype(F32) + last_ref[...].astype(F32)
        out_ref[:, :HD] = turn(total[:, :HD], cos_ref[...], -sin_ref[...]).astype(BF16)
        out_ref[:, HD:] = total[:, HD:].astype(BF16)

    (kv_grad,) = vmem_call(
        kv_body,
        [shape_of((count, kv_w), BF16)],
        [kv_close, kv_got, kv_last, cos_table, sin_table],
        0,
        blocks={0: (0, count), 1: (0, count)},
    )

    group_rows = n_y * n_x * width
    rows_of = lambda jy, jx: slice((jy * n_x + jx) * width, (jy * n_x + jx + 1) * width)

    def far_terms(grad, first_group, n_groups):
        def body(turned_ref, grad_ref, out_ref):
            out_ref[...] = matmul(turned_ref[...], grad_ref[...]).astype(BF16)

        rows = n_groups * group_rows
        return vmem_call(
            body,
            [shape_of((rows, grad.shape[1]), BF16)],
            [turned, grad],
            2 * rows * count * grad.shape[1],
            blocks={0: ((n_z + first_group) * group_rows, rows)},
        )[0]

    q_core = {jz: over_core(far_terms(q_grad, jz, 1)) for jz in (3, 2, 1, 0)}

    def x_terms(jz):
        def body(turned_ref, grad_ref, got_ref, out_ref):
            for jy in range(n_y):
                rows = rows_of(jy, 1)
                total = matmul(turned_ref[rows, :], grad_ref[...]) + got_ref[rows, :].astype(F32)
                out_ref[jy] = total.astype(BF16)

        return vmem_call(
            body,
            [shape_of((n_y, width, WQ), BF16)],
            [turned, q_grad, q_core[jz]],
            2 * n_y * width * count * WQ,
            blocks={0: (jz * group_rows, group_rows)},
        )[0]

    q_x = {jz: over_x(x_terms(jz)) for jz in (3, 2, 1, 0)}
    kv_core = over_core(far_terms(kv_grad, 0, n_z))

    def q_terms(jz, jy, added, dtype=BF16):
        def body(turned_ref, grad_ref, core_ref, x_ref, *refs):
            rows = rows_of(jy, 0)
            total = matmul(turned_ref[rows, :], grad_ref[...]) + core_ref[rows, :].astype(F32)
            total = total + x_ref[jy].astype(F32)
            for ref in refs[:-1]:
                total = total + ref[...].astype(F32)
            refs[-1][...] = total.astype(dtype)

        return vmem_call(
            body,
            [shape_of((width, WQ), dtype)],
            [turned, q_grad, q_core[jz], q_x[jz], *added],
            2 * width * count * WQ,
            blocks={0: (jz * group_rows, group_rows)},
        )[0]

    kv_wide = n_x * kv_w

    def kv_terms(z_list, jy, added, dtype=BF16):
        def body(turned_ref, grad_ref, core_ref, *refs):
            out_ref = refs[-1]
            for i, jz in enumerate(z_list):
                for jx in range(n_x):
                    at = (jz * n_y * n_x + jy * n_x + jx) * width
                    rows, cols = slice(at, at + width), slice(jx * kv_w, (jx + 1) * kv_w)
                    total = matmul(turned_ref[rows, :], grad_ref[...])
                    total = total + core_ref[rows, :].astype(F32)
                    for ref, (_, start) in zip(refs[:-1], added):
                        here = slice(start + i * width, start + (i + 1) * width)
                        total = total + ref[here, cols].astype(F32)
                    out_ref[i * width : (i + 1) * width, cols] = total.astype(dtype)

        return vmem_call(
            body,
            [shape_of((len(z_list) * width, kv_wide), dtype)],
            [turned, kv_grad, kv_core, *[array for array, _ in added]],
            2 * len(z_list) * width * count * kv_wide,
        )[0]

    kv_y = over_y(kv_terms(range(n_z), 1, []))
    q_y = {jz: over_y(q_terms(jz, 1, [])) for jz in (3, 2, 1, 0)}
    kv_z = {jz: over_z(kv_terms([jz], 0, [(kv_y, jz * width)]), jz) for jz in (3, 2, 1)}
    q_z = {jz: over_z(q_terms(jz, 0, [q_y[jz]]), jz) for jz in (3, 2, 1)}
    kv_sum = kv_terms([0], 0, [(kv_y, 0)] + [(a, 0) for a in kv_z.values()], F32)
    kv_other = over_x(kv_sum[:, kv_w:].astype(BF16))

    def sum_body(turned_ref, grad_ref, core_ref, x_ref, *refs):
        kv_ref, other_ref, out_ref = refs[-3:]
        rows = rows_of(0, 0)
        total = matmul(turned_ref[rows, :], grad_ref[...]) + core_ref[rows, :].astype(F32)
        total = total + x_ref[0].astype(F32)
        for ref in refs[:-3]:
            total = total + ref[...].astype(F32)
        out_ref[:, :WQ] = total
        out_ref[:, WQ:] = kv_ref[:, :kv_w] + other_ref[...].astype(F32)

    (grad_w,) = vmem_call(
        sum_body,
        [shape_of((width, WQ + kv_w), F32)],
        [turned, q_grad, q_core[0], q_x[0], q_y[0], *q_z.values(), kv_sum, kv_other],
        2 * width * count * WQ,
        blocks={0: (0, group_rows)},
    )

    keys = list(main)
    operands = [q_grad, kv_grad, w_qkv]
    operands += [mains[jc][k] for jc in range(n_core) for k in keys]
    at_side = len(operands)
    operands += [sides[jc][i] for jc in range(n_core) for i in range(len(groups))]

    def input_body(index_ref, *refs):
        row, col = index_ref[0], index_ref[1]
        out_ref = refs[-1]
        grad_q, grad_kv = refs[0][...], refs[1][...]
        n_k = n_core * n_x

        def put(jc, jz, jy, jx, value):
            place = (row ^ (jz * n_y + jy)) * n_k + (col ^ (jx * n_core + jc))
            at = pl.ds(pl.multiple_of(place * width, width), width)
            out_ref[:, at] = value.astype(BF16)

        mine = matmul(grad_q, refs[2][:, :WQ], 1, 1) + matmul(grad_kv, refs[2][:, WQ:], 1, 1)
        at = pl.ds(pl.multiple_of(row * (n_k * width), width), n_k * width)
        out_ref[:, at] = mine.astype(BF16)
        for jc in range(n_core):
            for g, group in enumerate(groups):
                x_ref = refs[at_side + jc * len(groups) + g]
                for i, (jz, jy) in enumerate(group):
                    ref = refs[3 + jc * len(keys) + keys.index((jz, jy))]
                    near = matmul(grad_q, ref[:, :WQ], 1, 1)
                    near = near + matmul(grad_kv, ref[:, WQ : WQ + kv_w], 1, 1)
                    put(jc, jz, jy, 0, near)
                    far = matmul(grad_q, x_ref[i], 1, 1)
                    far = far + matmul(grad_kv, ref[:, WQ + kv_w :], 1, 1)
                    put(jc, jz, jy, 1, far)

    (grad_inputs,) = vmem_call(
        input_body,
        [shape_of((count, features), BF16)],
        operands,
        2 * count * features * (WQ + kv_w),
        scalars=index,
    )
    return (attended[None], grad_inputs[None], grad_w)


def solution(mesh):
    in_specs = (
        P("dp", "ctx", None),
        P("dp", "ctx"),
        P("dp", "ctx"),
        P("dp", None),
        P("dp", "ctx", None),
    )
    out_specs = (P("dp", "ctx", None), P("dp", "ctx", None), P(("dp", "ctx"), None))
    n_dp, n_ctx = mesh.shape["dp"], mesh.shape["ctx"]
    near = (n_dp, n_ctx) == (8, 4)
    body = near_device if near else on_device
    return jax.shard_map(
        partial(body, n_dp, n_ctx),
        mesh=mesh,
        in_specs=in_specs,
        out_specs=out_specs,
        check_vma=False,
    )
```

profile of v0, /device:TPU:0, one launch (start us, length us, event | category | flops | bytes accessed | tf_op | source)
XLA Modules:
  0.0 126.6 jit_solution(14818803711613261022)
XLA Ops:
  4.6 4.1 %collective-permute-start.6 = (bf16[128,1024]{1,0:T(8,128)(2,1)S(1)}, bf16[128,1024]{1,0:T(8,128)(2,1)S(1)}, u32[]{:S(2)}, u32[]{:S(2)}) collective-permute-start(bf16[128,1024]{1,0:T(8,128)(2,1)S(1)} %pad_maximum_fusion), channel_id=1, source_target_pairs={{0,16},{4,20},{8,24},{12,28},{16,0},{20,4},{24,8},{28,12},{1,17},{... | collective-permute-start | bytes 786440 | tf_op jit(solution)/shard_map/ppermute | solution.py:54
  8.7 1.6 %collective-permute-start.4 = (bf16[128,1024]{1,0:T(8,128)(2,1)S(1)}, bf16[128,1024]{1,0:T(8,128)(2,1)S(1)}, u32[]{:S(2)}, u32[]{:S(2)}) collective-permute-start(bf16[128,1024]{1,0:T(8,128)(2,1)S(1)} %pad_maximum_fusion), channel_id=1, source_target_pairs={{0,8},{4,12},{8,0},{12,4},{16,24},{20,28},{24,16},{28,20},{1,9},{5... | collective-permute-start | bytes 786440 | tf_op jit(solution)/shard_map/ppermute | solution.py:54
  14.3 6.7 %collective-permute-done.4.refs_2_.refs_5_ = bf16[128,1024]{1,0:T(8,128)(2,1)S(1)} collective-permute-done((bf16[128,1024]{1,0:T(8,128)(2,1)S(1)}, bf16[128,1024]{1,0:T(8,128)(2,1)S(1)}, u32[]{:S(2)}, u32[]{:S(2)}) %collective-permute-start.4) | collective-permute-done | bytes 262176 | tf_op jit(solution)/shard_map/ppermute | solution.py:54
  21.1 1.5 %collective-permute-start.5 = (bf16[128,1024]{1,0:T(8,128)(2,1)S(1)}, bf16[128,1024]{1,0:T(8,128)(2,1)S(1)}, u32[]{:S(2)}, u32[]{:S(2)}) collective-permute-start(bf16[128,1024]{1,0:T(8,128)(2,1)S(1)} %collective-permute-done.4.refs_2_.refs_5_), channel_id=1, source_target_pairs={{0,4},{4,0},{8,12},{12,8},{16,20},{20,16},{24,28},{28,24},{1,5},{5... | collective-permute-start | bytes 786440 | tf_op jit(solution)/shard_map/ppermute | solution.py:54
  22.7 1.6 %collective-permute-start.8 = (bf16[2,128,512]{2,1,0:T(8,128)(2,1)S(1)}, bf16[2,128,512]{2,1,0:T(8,128)(2,1)S(1)}, u32[]{:S(2)}, u32[]{:S(2)}) collective-permute-start(bf16[2,128,512]{2,1,0:T(8,128)(2,1)S(1)} %pad_maximum_fusion.1), channel_id=1, source_target_pairs={{0,2},{1,3},{2,0},{3,1},{4,6},{5,7},{6,4},{7,5},{8,10},{9,11},{10,... | collective-permute-start | bytes 786440 | tf_op jit(solution)/shard_map/ppermute | solution.py:54
  24.8 2.8 %collective-permute-done.5.refs_3_.refs_6_ = bf16[128,1024]{1,0:T(8,128)(2,1)S(1)} collective-permute-done((bf16[128,1024]{1,0:T(8,128)(2,1)S(1)}, bf16[128,1024]{1,0:T(8,128)(2,1)S(1)}, u32[]{:S(2)}, u32[]{:S(2)}) %collective-permute-start.5) | collective-permute-done | bytes 262176 | tf_op jit(solution)/shard_map/ppermute | solution.py:54
  28.3 4.7 %collective-permute-done.7.refs_5_.refs_8_ = bf16[128,1024]{1,0:T(8,128)(2,1)S(1)} collective-permute-done((bf16[128,1024]{1,0:T(8,128)(2,1)S(1)}, bf16[128,1024]{1,0:T(8,128)(2,1)S(1)}, u32[]{:S(2)}, u32[]{:S(2)}) %collective-permute-start.7) | collective-permute-done | bytes 262176 | tf_op jit(solution)/shard_map/ppermute | solution.py:54
  33.1 1.5 %collective-permute-start.1 = (bf16[128,1024]{1,0:T(8,128)(2,1)S(1)}, bf16[128,1024]{1,0:T(8,128)(2,1)S(1)}, u32[]{:S(2)}, u32[]{:S(2)}) collective-permute-start(bf16[128,1024]{1,0:T(8,128)(2,1)S(1)} %collective-permute-done.refs_6_.refs_9_), channel_id=1, source_target_pairs={{0,4},{4,0},{8,12},{12,8},{16,20},{20,16},{24,28},{28,24},{1,5},{5... | collective-permute-start | bytes 786440 | tf_op jit(solution)/shard_map/ppermute | solution.py:54
  38.2 2.8 %collective-permute-done.1.refs_1_.refs_10_ = bf16[128,1024]{1,0:T(8,128)(2,1)S(1)} collective-permute-done((bf16[128,1024]{1,0:T(8,128)(2,1)S(1)}, bf16[128,1024]{1,0:T(8,128)(2,1)S(1)}, u32[]{:S(2)}, u32[]{:S(2)}) %collective-permute-start.1) | collective-permute-done | bytes 262176 | tf_op jit(solution)/shard_map/ppermute | solution.py:54
  43.0 2.5 %shard_map.77.refs_3_ = f32[256,768]{1,0:T(8,128)S(1)} custom-call(bf16[256,4096]{1,0:T(8,128)(2,1)S(1)} %get-tuple-element.12.refs_0_.refs_1_, bf16[128,1024]{1,0:T(8,128)(2,1)S(1)} %collective-permute-done.3.refs_1_.refs_4_, bf16[128,1024]{1,0:T(8,128)(2,1)S(1)} %collective-permute-done.4.refs_2_.refs_5_, ...), custom_call_target="tpu_custom_call" | custom-call | flops 1073741824 | bytes 8126464 | tf_op jit(solution)/shard_map/pallas_call | solution.py:262
  48.3 2.6 %collective-permute-done.18.refs_2_.refs_20_ = bf16[2,128,512]{2,1,0:T(8,128)(2,1)S(1)} collective-permute-done((bf16[2,128,512]{2,1,0:T(8,128)(2,1)S(1)}, bf16[2,128,512]{2,1,0:T(8,128)(2,1)S(1)}, u32[]{:S(2)}, u32[]{:S(2)}) %collective-permute-start.18) | collective-permute-done | bytes 262176 | tf_op jit(solution)/shard_map/ppermute | solution.py:54
  51.4 2.5 %collective-permute-done.22.refs_7_ = bf16[272,256]{1,0:T(8,128)(2,1)S(1)} collective-permute-done((bf16[272,256]{1,0:T(8,128)(2,1)S(1)}, bf16[272,256]{1,0:T(8,128)(2,1)S(1)}, u32[]{:S(2)}, u32[]{:S(2)}) %collective-permute-start.22) | collective-permute-done | bytes 139296 | tf_op jit(solution)/shard_map/ppermute | solution.py:54
  53.8 2.3 %collective-permute-done.19.refs_3_.refs_21_ = bf16[1,128,512]{2,1,0:T(8,128)(2,1)S(1)} collective-permute-done((bf16[1,128,512]{2,1,0:T(8,128)(2,1)S(1)}, bf16[1,128,512]{2,1,0:T(8,128)(2,1)S(1)}, u32[]{:S(2)}, u32[]{:S(2)}) %collective-permute-start.19) | collective-permute-done | bytes 131104 | tf_op jit(solution)/shard_map/ppermute | solution.py:54
  57.5 6.4 %shard_map.79 = (bf16[256,512]{1,0:T(8,128)(2,1)}, bf16[256,512]{1,0:T(8,128)(2,1)S(1)}, bf16[512,256]{1,0:T(8,128)(2,1)S(1)}, f32[512,256]{1,0:T(8,128)S(1)}) custom-call(f32[256,512]{1,0:T(8,128)S(1)} %get-tuple-element.14.refs_0_, bf16[256,4096]{1,0:T(8,128)(2,1)S(1)} %get-tuple-element.12.refs_0_.refs_1_, ...), custom_call_target="tpu_custom_call" | custom-call | flops 1879048192 | bytes 5799936 | tf_op jit(solution)/shard_map/pallas_call | solution.py:262
  66.8 4.3 %collective-permute-done.26.refs_2_ = bf16[256,256]{1,0:T(8,128)(2,1)S(1)} collective-permute-done((bf16[256,256]{1,0:T(8,128)(2,1)S(1)}, bf16[256,256]{1,0:T(8,128)(2,1)S(1)}, u32[]{:S(2)}, u32[]{:S(2)}) %collective-permute-start.26) | collective-permute-done | bytes 131104 | tf_op jit(solution)/shard_map/ppermute | solution.py:54
  81.6 4.2 %collective-permute-done.31.refs_3_ = bf16[2,128,512]{2,1,0:T(8,128)(2,1)S(1)} collective-permute-done((bf16[2,128,512]{2,1,0:T(8,128)(2,1)S(1)}, bf16[2,128,512]{2,1,0:T(8,128)(2,1)S(1)}, u32[]{:S(2)}, u32[]{:S(2)}) %collective-permute-start.31) | collective-permute-done | bytes 262176 | tf_op jit(solution)/shard_map/ppermute | solution.py:54
  86.8 4.6 %collective-permute-done.35.refs_3_ = bf16[2,128,512]{2,1,0:T(8,128)(2,1)S(1)} collective-permute-done((bf16[2,128,512]{2,1,0:T(8,128)(2,1)S(1)}, bf16[2,128,512]{2,1,0:T(8,128)(2,1)S(1)}, u32[]{:S(2)}, u32[]{:S(2)}) %collective-permute-start.35) | collective-permute-done | bytes 262176 | tf_op jit(solution)/shard_map/ppermute | solution.py:54
  92.4 4.6 %collective-permute-done.39.refs_3_ = bf16[2,128,512]{2,1,0:T(8,128)(2,1)S(1)} collective-permute-done((bf16[2,128,512]{2,1,0:T(8,128)(2,1)S(1)}, bf16[2,128,512]{2,1,0:T(8,128)(2,1)S(1)}, u32[]{:S(2)}, u32[]{:S(2)}) %collective-permute-start.39) | collective-permute-done | bytes 262176 | tf_op jit(solution)/shard_map/ppermute | solution.py:54
  98.2 2.3 %collective-permute-start.44 = (bf16[128,512]{1,0:T(8,128)(2,1)S(1)}, bf16[128,512]{1,0:T(8,128)(2,1)S(1)}, u32[]{:S(2)}, u32[]{:S(2)}) collective-permute-start(bf16[128,512]{1,0:T(8,128)(2,1)S(1)} %shard_map.100), channel_id=1, source_target_pairs={{0,24},{4,28},{8,16},{12,20},{16,8},{20,12},{24,0},{28,4},{1,25},{... | collective-permute-start | bytes 393224 | tf_op jit(solution)/shard_map/ppermute | solution.py:54
  101.7 2.3 %collective-permute-start.45 = (bf16[128,512]{1,0:T(8,128)(2,1)S(1)}, bf16[128,512]{1,0:T(8,128)(2,1)S(1)}, u32[]{:S(2)}, u32[]{:S(2)}) collective-permute-start(bf16[128,512]{1,0:T(8,128)(2,1)S(1)} %shard_map.101), channel_id=1, source_target_pairs={{0,16},{4,20},{8,24},{12,28},{16,0},{20,4},{24,8},{28,12},{1,17},{... | collective-permute-start | bytes 393224 | tf_op jit(solution)/shard_map/ppermute | solution.py:54
  106.2 1.8 %collective-permute-start.33 = (bf16[128,512]{1,0:T(8,128)(2,1)S(1)}, bf16[128,512]{1,0:T(8,128)(2,1)S(1)}, u32[]{:S(2)}, u32[]{:S(2)}) collective-permute-start(bf16[128,512]{1,0:T(8,128)(2,1)S(1)} %shard_map.89), channel_id=1, source_target_pairs={{0,24},{4,28},{8,16},{12,20},{16,8},{20,12},{24,0},{28,4},{1,25},{... | collective-permute-start | bytes 393224 | tf_op jit(solution)/shard_map/ppermute | solution.py:54
  108.3 4.8 %collective-permute-start.37 = (bf16[128,512]{1,0:T(8,128)(2,1)S(1)}, bf16[128,512]{1,0:T(8,128)(2,1)S(1)}, u32[]{:S(2)}, u32[]{:S(2)}) collective-permute-start(bf16[128,512]{1,0:T(8,128)(2,1)S(1)} %shard_map.93), channel_id=1, source_target_pairs={{0,16},{4,20},{8,24},{12,28},{16,0},{20,4},{24,8},{28,12},{1,17},{... | collective-permute-start | bytes 393224 | tf_op jit(solution)/shard_map/ppermute | solution.py:54
  113.1 6.0 %collective-permute-done.45.refs_5_ = bf16[128,512]{1,0:T(8,128)(2,1)S(1)} collective-permute-done((bf16[128,512]{1,0:T(8,128)(2,1)S(1)}, bf16[128,512]{1,0:T(8,128)(2,1)S(1)}, u32[]{:S(2)}, u32[]{:S(2)}) %collective-permute-start.45) | collective-permute-done | bytes 131104 | tf_op jit(solution)/shard_map/ppermute | solution.py:54
  120.2 5.3 %shard_map.82 = bf16[256,4096]{1,0:T(8,128)(2,1)} custom-call(s32[2]{0:T(128)S(1)} %pad_add_fusion.refs_0_, bf16[256,512]{1,0:T(8,128)(2,1)S(1)} %get-tuple-element.17.refs_1_, bf16[256,256]{1,0:T(8,128)(2,1)S(1)} %shard_map.81.refs_2_.refs_1_, bf16[512,768]{1,0:T(8,128)(2,1)S(1)} %copy-done, bf16[128,1024]{1,0:T(8,128)(2,1)S(1)} %collective-permute-done.3.refs_1_.refs_4_, ...), custom_call_target="tpu_custom_call" | custom-call | flops 1610612736 | bytes 8781824 | tf_op jit(solution)/shard_map/pallas_call | solution.py:262
  (134 shorter events, 40.2 us)
Async XLA Ops:
  4.6 19.6 %collective-permute-start.6 = (bf16[128,1024]{1,0:T(8,128)(2,1)S(1)}, bf16[128,1024]{1,0:T(8,128)(2,1)S(1)}, u32[]{:S(2)}, u32[]{:S(2)}) collective-permute-start(bf16[128,1024]{1,0:T(8,128)(2,1)S(1)} %pad_maximum_fusion), channel_id=1, source_target_pairs={{0,16},{4,20},{8,24},{12,28},{16,0},{20,4},{24,8},{28,12},{1,17},{... | collective-permute-start | bytes 786440 | tf_op jit(solution)/shard_map/ppermute | solution.py:54
  8.7 12.4 %collective-permute-start.4 = (bf16[128,1024]{1,0:T(8,128)(2,1)S(1)}, bf16[128,1024]{1,0:T(8,128)(2,1)S(1)}, u32[]{:S(2)}, u32[]{:S(2)}) collective-permute-start(bf16[128,1024]{1,0:T(8,128)(2,1)S(1)} %pad_maximum_fusion), channel_id=1, source_target_pairs={{0,8},{4,12},{8,0},{12,4},{16,24},{20,28},{24,16},{28,20},{1,9},{5... | collective-permute-start | bytes 786440 | tf_op jit(solution)/shard_map/ppermute | solution.py:54
  10.3 12.3 %collective-permute-start.3 = (bf16[128,1024]{1,0:T(8,128)(2,1)S(1)}, bf16[128,1024]{1,0:T(8,128)(2,1)S(1)}, u32[]{:S(2)}, u32[]{:S(2)}) collective-permute-start(bf16[128,1024]{1,0:T(8,128)(2,1)S(1)} %pad_maximum_fusion), channel_id=1, source_target_pairs={{0,4},{4,0},{8,12},{12,8},{16,20},{20,16},{24,28},{28,24},{1,5},{5... | collective-permute-start | bytes 786440 | tf_op jit(solution)/shard_map/ppermute | solution.py:54
  11.8 15.9 %collective-permute-start = (bf16[128,1024]{1,0:T(8,128)(2,1)S(1)}, bf16[128,1024]{1,0:T(8,128)(2,1)S(1)}, u32[]{:S(2)}, u32[]{:S(2)}) collective-permute-start(bf16[128,1024]{1,0:T(8,128)(2,1)S(1)} %pad_maximum_fusion), channel_id=1, source_target_pairs={{0,24},{4,28},{8,16},{12,20},{16,8},{20,12},{24,0},{28,4},{1,25},{... | collective-permute-start | bytes 786440 | tf_op jit(solution)/shard_map/ppermute | solution.py:54
  22.7 14.9 %collective-permute-start.8 = (bf16[2,128,512]{2,1,0:T(8,128)(2,1)S(1)}, bf16[2,128,512]{2,1,0:T(8,128)(2,1)S(1)}, u32[]{:S(2)}, u32[]{:S(2)}) collective-permute-start(bf16[2,128,512]{2,1,0:T(8,128)(2,1)S(1)} %pad_maximum_fusion.1), channel_id=1, source_target_pairs={{0,2},{1,3},{2,0},{3,1},{4,6},{5,7},{6,4},{7,5},{8,10},{9,11},{10,... | collective-permute-start | bytes 786440 | tf_op jit(solution)/shard_map/ppermute | solution.py:54
  24.2 8.8 %collective-permute-start.7 = (bf16[128,1024]{1,0:T(8,128)(2,1)S(1)}, bf16[128,1024]{1,0:T(8,128)(2,1)S(1)}, u32[]{:S(2)}, u32[]{:S(2)}) collective-permute-start(bf16[128,1024]{1,0:T(8,128)(2,1)S(1)} %collective-permute-done.6.refs_4_.refs_7_), channel_id=1, source_target_pairs={{0,4},{4,0},{8,12},{12,8},{16,20},{20,16},{24,28},{28,24},{1,5},{5... | collective-permute-start | bytes 786440 | tf_op jit(solution)/shard_map/ppermute | solution.py:54
  27.7 9.9 %collective-permute-start.10 = (bf16[128,1024]{1,0:T(8,128)(2,1)S(1)}, bf16[128,1024]{1,0:T(8,128)(2,1)S(1)}, u32[]{:S(2)}, u32[]{:S(2)}) collective-permute-start(bf16[128,1024]{1,0:T(8,128)(2,1)S(1)} %collective-permute-done.3.refs_1_.refs_4_), channel_id=1, source_target_pairs={{0,1},{1,0},{2,3},{3,2},{4,5},{5,4},{6,7},{7,6},{8,9},{9,8},{10,11... | collective-permute-start | bytes 786440 | tf_op jit(solution)/shard_map/ppermute | solution.py:54
  28.3 9.9 %collective-permute-start.15 = (bf16[128,1024]{1,0:T(8,128)(2,1)S(1)}, bf16[128,1024]{1,0:T(8,128)(2,1)S(1)}, u32[]{:S(2)}, u32[]{:S(2)}) collective-permute-start(bf16[128,1024]{1,0:T(8,128)(2,1)S(1)} %collective-permute-done.refs_6_.refs_9_), channel_id=1, source_target_pairs={{0,1},{1,0},{2,3},{3,2},{4,5},{5,4},{6,7},{7,6},{8,9},{9,8},{10,11... | collective-permute-start | bytes 786440 | tf_op jit(solution)/shard_map/ppermute | solution.py:54
  41.6 9.2 %collective-permute-start.18 = (bf16[2,128,512]{2,1,0:T(8,128)(2,1)S(1)}, bf16[2,128,512]{2,1,0:T(8,128)(2,1)S(1)}, u32[]{:S(2)}, u32[]{:S(2)}) collective-permute-start(bf16[2,128,512]{2,1,0:T(8,128)(2,1)S(1)} %pad_maximum_fusion.3), channel_id=1, source_target_pairs={{0,2},{1,3},{2,0},{3,1},{4,6},{5,7},{6,4},{7,5},{8,10},{9,11},{10,... | collective-permute-start | bytes 786440 | tf_op jit(solution)/shard_map/ppermute | solution.py:54
  47.4 8.8 %collective-permute-start.19 = (bf16[1,128,512]{2,1,0:T(8,128)(2,1)S(1)}, bf16[1,128,512]{2,1,0:T(8,128)(2,1)S(1)}, u32[]{:S(2)}, u32[]{:S(2)}) collective-permute-start(bf16[1,128,512]{2,1,0:T(8,128)(2,1)S(1)} %slice_bitcast_fusion), channel_id=1, source_target_pairs={{0,2},{1,3},{2,0},{3,1},{4,6},{5,7},{6,4},{7,5},{8,10},{9,11},{10,... | collective-permute-start | bytes 393224 | tf_op jit(solution)/shard_map/ppermute | solution.py:54
  74.9 23.1 %collective-permute-start.43 = (bf16[512,512]{1,0:T(8,128)(2,1)S(1)}, bf16[512,512]{1,0:T(8,128)(2,1)S(1)}, u32[]{:S(2)}, u32[]{:S(2)}) collective-permute-start(bf16[512,512]{1,0:T(8,128)(2,1)S(1)} %shard_map.99), channel_id=1, source_target_pairs={{0,4},{4,0},{8,12},{12,8},{16,20},{20,16},{24,28},{28,24},{1,5},{5... | collective-permute-start | bytes 1572872 | tf_op jit(solution)/shard_map/ppermute | solution.py:54
  76.5 9.2 %collective-permute-start.31 = (bf16[2,128,512]{2,1,0:T(8,128)(2,1)S(1)}, bf16[2,128,512]{2,1,0:T(8,128)(2,1)S(1)}, u32[]{:S(2)}, u32[]{:S(2)}) collective-permute-start(bf16[2,128,512]{2,1,0:T(8,128)(2,1)S(1)} %shard_map.87), channel_id=1, source_target_pairs={{0,2},{1,3},{2,0},{3,1},{4,6},{5,7},{6,4},{7,5},{8,10},{9,11},{10,... | collective-permute-start | bytes 786440 | tf_op jit(solution)/shard_map/ppermute | solution.py:54
  77.6 13.8 %collective-permute-start.35 = (bf16[2,128,512]{2,1,0:T(8,128)(2,1)S(1)}, bf16[2,128,512]{2,1,0:T(8,128)(2,1)S(1)}, u32[]{:S(2)}, u32[]{:S(2)}) collective-permute-start(bf16[2,128,512]{2,1,0:T(8,128)(2,1)S(1)} %shard_map.91), channel_id=1, source_target_pairs={{0,2},{1,3},{2,0},{3,1},{4,6},{5,7},{6,4},{7,5},{8,10},{9,11},{10,... | collective-permute-start | bytes 786440 | tf_op jit(solution)/shard_map/ppermute | solution.py:54
  79.2 17.8 %collective-permute-start.39 = (bf16[2,128,512]{2,1,0:T(8,128)(2,1)S(1)}, bf16[2,128,512]{2,1,0:T(8,128)(2,1)S(1)}, u32[]{:S(2)}, u32[]{:S(2)}) collective-permute-start(bf16[2,128,512]{2,1,0:T(8,128)(2,1)S(1)} %shard_map.95), channel_id=1, source_target_pairs={{0,2},{1,3},{2,0},{3,1},{4,6},{5,7},{6,4},{7,5},{8,10},{9,11},{10,... | collective-permute-start | bytes 786440 | tf_op jit(solution)/shard_map/ppermute | solution.py:54
  80.2 21.4 %collective-permute-start.28 = (bf16[2,128,512]{2,1,0:T(8,128)(2,1)S(1)}, bf16[2,128,512]{2,1,0:T(8,128)(2,1)S(1)}, u32[]{:S(2)}, u32[]{:S(2)}) collective-permute-start(bf16[2,128,512]{2,1,0:T(8,128)(2,1)S(1)} %shard_map.84), channel_id=1, source_target_pairs={{0,2},{1,3},{2,0},{3,1},{4,6},{5,7},{6,4},{7,5},{8,10},{9,11},{10,... | collective-permute-start | bytes 786440 | tf_op jit(solution)/shard_map/ppermute | solution.py:54
  86.0 18.1 %collective-permute-start.32 = (bf16[128,512]{1,0:T(8,128)(2,1)S(1)}, bf16[128,512]{1,0:T(8,128)(2,1)S(1)}, u32[]{:S(2)}, u32[]{:S(2)}) collective-permute-start(bf16[128,512]{1,0:T(8,128)(2,1)S(1)} %shard_map.88), channel_id=1, source_target_pairs={{0,4},{4,0},{8,12},{12,8},{16,20},{20,16},{24,28},{28,24},{1,5},{5... | collective-permute-start | bytes 393224 | tf_op jit(solution)/shard_map/ppermute | solution.py:54
  91.6 13.0 %collective-permute-start.36 = (bf16[128,512]{1,0:T(8,128)(2,1)S(1)}, bf16[128,512]{1,0:T(8,128)(2,1)S(1)}, u32[]{:S(2)}, u32[]{:S(2)}) collective-permute-start(bf16[128,512]{1,0:T(8,128)(2,1)S(1)} %shard_map.92), channel_id=1, source_target_pairs={{0,4},{4,0},{8,12},{12,8},{16,20},{20,16},{24,28},{28,24},{1,5},{5... | collective-permute-start | bytes 393224 | tf_op jit(solution)/shard_map/ppermute | solution.py:54
  97.2 9.0 %collective-permute-start.40 = (bf16[128,512]{1,0:T(8,128)(2,1)S(1)}, bf16[128,512]{1,0:T(8,128)(2,1)S(1)}, u32[]{:S(2)}, u32[]{:S(2)}) collective-permute-start(bf16[128,512]{1,0:T(8,128)(2,1)S(1)} %shard_map.96), channel_id=1, source_target_pairs={{0,4},{4,0},{8,12},{12,8},{16,20},{20,16},{24,28},{28,24},{1,5},{5... | collective-permute-start | bytes 393224 | tf_op jit(solution)/shard_map/ppermute | solution.py:54
  98.2 10.0 %collective-permute-start.44 = (bf16[128,512]{1,0:T(8,128)(2,1)S(1)}, bf16[128,512]{1,0:T(8,128)(2,1)S(1)}, u32[]{:S(2)}, u32[]{:S(2)}) collective-permute-start(bf16[128,512]{1,0:T(8,128)(2,1)S(1)} %shard_map.100), channel_id=1, source_target_pairs={{0,24},{4,28},{8,16},{12,20},{16,8},{20,12},{24,0},{28,4},{1,25},{... | collective-permute-start | bytes 393224 | tf_op jit(solution)/shard_map/ppermute | solution.py:54
  101.7 17.4 %collective-permute-start.45 = (bf16[128,512]{1,0:T(8,128)(2,1)S(1)}, bf16[128,512]{1,0:T(8,128)(2,1)S(1)}, u32[]{:S(2)}, u32[]{:S(2)}) collective-permute-start(bf16[128,512]{1,0:T(8,128)(2,1)S(1)} %shard_map.101), channel_id=1, source_target_pairs={{0,16},{4,20},{8,24},{12,28},{16,0},{20,4},{24,8},{28,12},{1,17},{... | collective-permute-start | bytes 393224 | tf_op jit(solution)/shard_map/ppermute | solution.py:54
  104.0 15.0 %collective-permute-start.46 = (bf16[128,512]{1,0:T(8,128)(2,1)S(1)}, bf16[128,512]{1,0:T(8,128)(2,1)S(1)}, u32[]{:S(2)}, u32[]{:S(2)}) collective-permute-start(bf16[128,512]{1,0:T(8,128)(2,1)S(1)} %shard_map.102), channel_id=1, source_target_pairs={{0,8},{4,12},{8,0},{12,4},{16,24},{20,28},{24,16},{28,20},{1,9},{5... | collective-permute-start | bytes 393224 | tf_op jit(solution)/shard_map/ppermute | solution.py:54
  104.6 21.0 %collective-permute-start.29 = (bf16[128,512]{1,0:T(8,128)(2,1)S(1)}, bf16[128,512]{1,0:T(8,128)(2,1)S(1)}, u32[]{:S(2)}, u32[]{:S(2)}) collective-permute-start(bf16[128,512]{1,0:T(8,128)(2,1)S(1)} %shard_map.85), channel_id=1, source_target_pairs={{0,4},{4,0},{8,12},{12,8},{16,20},{20,16},{24,28},{28,24},{1,5},{5... | collective-permute-start | bytes 393224 | tf_op jit(solution)/shard_map/ppermute | solution.py:54
  106.2 19.4 %collective-permute-start.33 = (bf16[128,512]{1,0:T(8,128)(2,1)S(1)}, bf16[128,512]{1,0:T(8,128)(2,1)S(1)}, u32[]{:S(2)}, u32[]{:S(2)}) collective-permute-start(bf16[128,512]{1,0:T(8,128)(2,1)S(1)} %shard_map.89), channel_id=1, source_target_pairs={{0,24},{4,28},{8,16},{12,20},{16,8},{20,12},{24,0},{28,4},{1,25},{... | collective-permute-start | bytes 393224 | tf_op jit(solution)/shard_map/ppermute | solution.py:54
  108.3 17.3 %collective-permute-start.37 = (bf16[128,512]{1,0:T(8,128)(2,1)S(1)}, bf16[128,512]{1,0:T(8,128)(2,1)S(1)}, u32[]{:S(2)}, u32[]{:S(2)}) collective-permute-start(bf16[128,512]{1,0:T(8,128)(2,1)S(1)} %shard_map.93), channel_id=1, source_target_pairs={{0,16},{4,20},{8,24},{12,28},{16,0},{20,4},{24,8},{28,12},{1,17},{... | collective-permute-start | bytes 393224 | tf_op jit(solution)/shard_map/ppermute | solution.py:54
  (27 other events, 181.6 us)
where the time goes:
time: 127 us
  waiting for transfers between devices  52.7 us (41%)
  starting transfers between devices  43.9 us (35%)
  Pallas kernels  22.4 us (18%)
  local copies, waits for them, and re-layouts  2.79 us (2%)
  other arithmetic  2.43 us (2%)
  between operations  2.39 us (2%)
    ppermute x48, waiting for transfers between devices, exchange(): return lax.ppermute(array, axis, [(i, i ^ offset) for i in range(size)])  52.7 us
    ppermute x48, starting transfers between devices, exchange(): return lax.ppermute(array, axis, [(i, i ^ offset) for i in range(size)])  43.9 us
    pallas_call x29, Pallas kernels, vmem_call(): pl.pallas_call(cut_body, out_shape=out_shapes, in_specs=[pl.BlockSpec(mem...  22.4 us
  transfers between devices with their start and end apart: 48, of which 18 were waited for; matrix products, arithmetic and copies ran while one was open for 2% of the time, Pallas kernels for 11%

commit v1 on v0

--- a/solution.py
+++ b/solution.py
@@ -401,9 +401,10 @@
     n_core, n_x, n_z = 2, 2, 4
     n_y = n_dp // n_z
     dims = (n_core, n_x, n_y, n_z)
-    index = jnp.stack([lax.axis_index("dp"), lax.axis_index("ctx")]).astype(jnp.int32)
-    index = lax.optimization_barrier(index)
-    col = index[1]
+    row, col = lax.optimization_barrier(
+        (lax.axis_index("dp").astype(jnp.int32), lax.axis_index("ctx").astype(jnp.int32))
+    )
+    index = jnp.stack([row, col])
     shard = w_qkv.shape[0]
     width = shard // n_ctx
     kv_w = 2 * HD
@@ -418,7 +419,8 @@
     own_rows = lax.dynamic_slice_in_dim(w_qkv, col * width, width, 0)
     other_rows = lax.dynamic_slice_in_dim(w_qkv, (col ^ n_core) * width, width, 0)
     piece = jnp.concatenate([own_rows, other_rows[:, WQ:]], axis=1)
-    by_z = {o: over_z(piece, o) for o in (1, 2, 3)}
+    by_z = {o: over_z(piece, o) for o in (1, 2)}
+    by_z[3] = over_z(by_z[2], 1)
     by_y = {0: over_y(piece)}
     for o in (1, 2, 3):
         by_y[o] = over_y(by_z[o])
@@ -427,7 +429,15 @@
         main[(o, 0)] = by_z[o]
         main[(o, 1)] = by_y[o]
     groups = [[(0, 1), (1, 0)], [(1, 1), (2, 0)], [(2, 1), (3, 0)], [(3, 1)]]
-    side = [over_x(jnp.stack([main[k][:, :WQ] for k in group])) for group in groups]
+
+    def pack(arrays):
+        def body(*refs):
+            for j, ref in enumerate(refs[:-1]):
+                refs[-1][j] = ref[:, :WQ]
+
+        return vmem_call(body, [shape_of((len(arrays), width, WQ), BF16)], arrays, 0)[0]
+
+    side = [over_x(pack([main[k] for k in group])) for group in groups]
     mains = [main, {k: over_core(a) for k, a in main.items()}]
     sides = [side, [over_core(a) for a in side]]
 
@@ -563,7 +573,7 @@
             blocks={0: ((n_z + first_group) * group_rows, rows)},
         )[0]
 
-    q_core = {jz: over_core(far_terms(q_grad, jz, 1)) for jz in (3, 2, 1, 0)}
+    q_core = {jz: over_core(far_terms(q_grad, jz, 1)) for jz in (3, 1, 2, 0)}
 
     def x_terms(jz):
         def body(turned_ref, grad_ref, got_ref, out_ref):
@@ -580,24 +590,30 @@
             blocks={0: (jz * group_rows, group_rows)},
         )[0]
 
-    q_x = {jz: over_x(x_terms(jz)) for jz in (3, 2, 1, 0)}
+    q_x = {jz: over_x(x_terms(jz)) for jz in (3, 1, 2, 0)}
     kv_core = over_core(far_terms(kv_grad, 0, n_z))
 
-    def q_terms(jz, jy, added, dtype=BF16):
-        def body(turned_ref, grad_ref, core_ref, x_ref, *refs):
-            rows = rows_of(jy, 0)
-            total = matmul(turned_ref[rows, :], grad_ref[...]) + core_ref[rows, :].astype(F32)
-            total = total + x_ref[jy].astype(F32)
-            for ref in refs[:-1]:
-                total = total + ref[...].astype(F32)
-            refs[-1][...] = total.astype(dtype)
-
+    def q_terms(z_list, jy, added):
+        n_z_list = len(z_list)
+
+        def body(turned_ref, grad_ref, *refs):
+            core_refs, x_refs = refs[:n_z_list], refs[n_z_list : 2 * n_z_list]
+            for i, jz in enumerate(z_list):
+                rows = rows_of(jy, 0)
+                at = jz * group_rows + rows.start
+                total = matmul(turned_ref[at : at + width, :], grad_ref[...])
+                total = total + core_refs[i][rows, :].astype(F32) + x_refs[i][jy].astype(F32)
+                for ref, (_, pick, start) in zip(refs[2 * n_z_list : -1], added):
+                    if pick == jz:
+                        total = total + ref[start : start + width, :].astype(F32)
+                refs[-1][i * width : (i + 1) * width, :] = total.astype(BF16)
+
+        operands = [turned, q_grad] + [q_core[jz] for jz in z_list] + [q_x[jz] for jz in z_list]
         return vmem_call(
             body,
-            [shape_of((width, WQ), dtype)],
-            [turned, q_grad, q_core[jz], q_x[jz], *added],
-            2 * width * count * WQ,
-            blocks={0: (jz * group_rows, group_rows)},
+            [shape_of((n_z_list * width, WQ), BF16)],
+            operands + [array for array, _, _ in added],
+            2 * n_z_list * width * count * WQ,
         )[0]
 
     kv_wide = n_x * kv_w
@@ -623,27 +639,31 @@
             2 * len(z_list) * width * count * kv_wide,
         )[0]
 
-    kv_y = over_y(kv_terms(range(n_z), 1, []))
-    q_y = {jz: over_y(q_terms(jz, 1, [])) for jz in (3, 2, 1, 0)}
-    kv_z = {jz: over_z(kv_terms([jz], 0, [(kv_y, jz * width)]), jz) for jz in (3, 2, 1)}
-    q_z = {jz: over_z(q_terms(jz, 0, [q_y[jz]]), jz) for jz in (3, 2, 1)}
-    kv_sum = kv_terms([0], 0, [(kv_y, 0)] + [(a, 0) for a in kv_z.values()], F32)
+    kv_y31 = over_y(kv_terms([3, 1], 1, []))
+    kv_y20 = over_y(kv_terms([2, 0], 1, []))
+    q_y = {jz: over_y(q_terms([jz], 1, [])) for jz in (3, 1, 2, 0)}
+    kv_z31 = over_z(kv_terms([3, 1], 0, [(kv_y31, 0)]), 1)
+    kv_z2 = over_z(kv_terms([2], 0, [(kv_y20, 0), (kv_z31, 0)]), 2)
+    q_z31 = q_terms([3, 1], 0, [(q_y[3], 3, 0), (q_y[1], 1, 0)])
+    q_z31 = over_z(q_z31, 1)
+    q_z2 = q_terms([2], 0, [(q_y[2], 2, 0), (q_z31, 2, 0)])
+    q_z2 = over_z(q_z2, 2)
+    kv_sum = kv_terms([0], 0, [(kv_y20, width), (kv_z31, width), (kv_z2, 0)], F32)
     kv_other = over_x(kv_sum[:, kv_w:].astype(BF16))
 
-    def sum_body(turned_ref, grad_ref, core_ref, x_ref, *refs):
-        kv_ref, other_ref, out_ref = refs[-3:]
+    def sum_body(turned_ref, grad_ref, core_ref, x_ref, y_ref, z_ref, z2_ref, *refs):
+        kv_ref, other_ref, out_ref = refs
         rows = rows_of(0, 0)
         total = matmul(turned_ref[rows, :], grad_ref[...]) + core_ref[rows, :].astype(F32)
         total = total + x_ref[0].astype(F32)
-        for ref in refs[:-3]:
-            total = total + ref[...].astype(F32)
-        out_ref[:, :WQ] = total
+        total = total + y_ref[...].astype(F32) + z_ref[width:, :].astype(F32)
+        out_ref[:, :WQ] = total + z2_ref[...].astype(F32)
         out_ref[:, WQ:] = kv_ref[:, :kv_w] + other_ref[...].astype(F32)
 
     (grad_w,) = vmem_call(
         sum_body,
         [shape_of((width, WQ + kv_w), F32)],
-        [turned, q_grad, q_core[0], q_x[0], q_y[0], *q_z.values(), kv_sum, kv_other],
+        [turned, q_grad, q_core[0], q_x[0], q_y[0], q_z31, q_z2, kv_sum, kv_other],
         2 * width * count * WQ,
         blocks={0: (0, group_rows)},
     )

time: 127 us -> 116 us (0.913)
  waiting for transfers between devices: 52.7 us -> 41.9 us
  starting transfers between devices: 43.9 us -> 46.6 us
  between operations: 2.39 us -> 1.07 us
    ppermute x48 -> x47, waiting for transfers between devices: 52.7 us -> 41.9 us  [exchange(): return lax.ppermute(array, axis, [(i, i ^ offset) for i in range(size)])]
    ppermute x48 -> x47, starting transfers between devices: 43.9 us -> 46.6 us  [exchange(): return lax.ppermute(array, axis, [(i, i ^ offset) for i in range(size)])]
    pallas_call x29 -> x32, Pallas kernels: 22.4 us -> 22.3 us  [vmem_call(): pl.pallas_call(cut_body, out_shape=out_shapes, in_specs=[pl.BlockSpec(mem...]
  transfers between devices with their start and end apart: 48 -> 47, of which waited for: 18 -> 17; matrix products, arithmetic and copies ran while one was open for 2% -> 2% of each run, Pallas kernels for 11% -> 12%
where the time goes in v1:
time: 116 us
  starting transfers between devices  46.6 us (40%)
  waiting for transfers between devices  41.9 us (36%)
  Pallas kernels  22.3 us (19%)
  local copies, waits for them, and re-layouts  2.13 us (2%)
  other arithmetic  1.65 us (1%)
    ppermute x47, starting transfers between devices, exchange(): return lax.ppermute(array, axis, [(i, i ^ offset) for i in range(size)])  46.6 us
    ppermute x47, waiting for transfers between devices, exchange(): return lax.ppermute(array, axis, [(i, i ^ offset) for i in range(size)])  41.9 us
    pallas_call x32, Pallas kernels, vmem_call(): pl.pallas_call(cut_body, out_shape=out_shapes, in_specs=[pl.BlockSpec(mem...  22.3 us
  transfers between devices with their start and end apart: 47, of which 17 were waited for; matrix products, arithmetic and copies ran while one was open for 2% of the time, Pallas kernels for 12%

profile of v1, /device:TPU:0, one launch (start us, length us, event | category | flops | bytes accessed | tf_op | source)
XLA Modules:
  0.0 115.7 jit_solution(8310929757078486118)
XLA Ops:
  2.6 3.1 %collective-permute-start.5 = (bf16[128,1024]{1,0:T(8,128)(2,1)S(1)}, bf16[128,1024]{1,0:T(8,128)(2,1)S(1)}, u32[]{:S(2)}, u32[]{:S(2)}) collective-permute-start(bf16[128,1024]{1,0:T(8,128)(2,1)S(1)} %pad_maximum_fusion), channel_id=1, source_target_pairs={{0,8},{4,12},{8,0},{12,4},{16,24},{20,28},{24,16},{28,20},{1,9},{5... | collective-permute-start | bytes 786440 | tf_op jit(solution)/shard_map/ppermute | solution.py:54
  7.3 2.6 %collective-permute-start = (bf16[128,1024]{1,0:T(8,128)(2,1)S(1)}, bf16[128,1024]{1,0:T(8,128)(2,1)S(1)}, u32[]{:S(2)}, u32[]{:S(2)}) collective-permute-start(bf16[128,1024]{1,0:T(8,128)(2,1)S(1)} %pad_maximum_fusion), channel_id=1, source_target_pairs={{0,16},{4,20},{8,24},{12,28},{16,0},{20,4},{24,8},{28,12},{1,17},{... | collective-permute-start | bytes 786440 | tf_op jit(solution)/shard_map/ppermute | solution.py:54
  9.9 6.5 %collective-permute-done.5.refs_1_.refs_2_.refs_5_ = bf16[128,1024]{1,0:T(8,128)(2,1)S(1)} collective-permute-done((bf16[128,1024]{1,0:T(8,128)(2,1)S(1)}, bf16[128,1024]{1,0:T(8,128)(2,1)S(1)}, u32[]{:S(2)}, u32[]{:S(2)}) %collective-permute-start.5) | collective-permute-done | bytes 262176 | tf_op jit(solution)/shard_map/ppermute | solution.py:54
  16.3 2.7 %collective-permute-start.6 = (bf16[128,1024]{1,0:T(8,128)(2,1)S(1)}, bf16[128,1024]{1,0:T(8,128)(2,1)S(1)}, u32[]{:S(2)}, u32[]{:S(2)}) collective-permute-start(bf16[128,1024]{1,0:T(8,128)(2,1)S(1)} %collective-permute-done.5.refs_1_.refs_2_.refs_5_), channel_id=1, source_target_pairs={{0,4},{4,0},{8,12},{12,8},{16,20},{20,16},{24,28},{28,24},{1,5},{5... | collective-permute-start | bytes 786440 | tf_op jit(solution)/shard_map/ppermute | solution.py:54
  19.8 1.6 %collective-permute-start.8 = (bf16[2,128,512]{2,1,0:T(8,128)(2,1)S(1)}, bf16[2,128,512]{2,1,0:T(8,128)(2,1)S(1)}, u32[]{:S(2)}, u32[]{:S(2)}) collective-permute-start(bf16[2,128,512]{2,1,0:T(8,128)(2,1)S(1)} %shard_map.77), channel_id=1, source_target_pairs={{0,2},{1,3},{2,0},{3,1},{4,6},{5,7},{6,4},{7,5},{8,10},{9,11},{10,... | collective-permute-start | bytes 786440 | tf_op jit(solution)/shard_map/ppermute | solution.py:54
  21.9 2.5 %collective-permute-done.6.refs_0_.refs_3_.refs_6_ = bf16[128,1024]{1,0:T(8,128)(2,1)S(1)} collective-permute-done((bf16[128,1024]{1,0:T(8,128)(2,1)S(1)}, bf16[128,1024]{1,0:T(8,128)(2,1)S(1)}, u32[]{:S(2)}, u32[]{:S(2)}) %collective-permute-start.6) | collective-permute-done | bytes 262176 | tf_op jit(solution)/shard_map/ppermute | solution.py:54
  24.5 1.8 %collective-permute-start.7 = (bf16[128,1024]{1,0:T(8,128)(2,1)S(1)}, bf16[128,1024]{1,0:T(8,128)(2,1)S(1)}, u32[]{:S(2)}, u32[]{:S(2)}) collective-permute-start(bf16[128,1024]{1,0:T(8,128)(2,1)S(1)} %collective-permute-done.refs_1_.refs_4_.refs_7_), channel_id=1, source_target_pairs={{0,4},{4,0},{8,12},{12,8},{16,20},{20,16},{24,28},{28,24},{1,5},{5... | collective-permute-start | bytes 786440 | tf_op jit(solution)/shard_map/ppermute | solution.py:54
  29.4 1.7 %collective-permute-done.1.refs_6_.refs_1_.refs_9_ = bf16[128,1024]{1,0:T(8,128)(2,1)S(1)} collective-permute-done((bf16[128,1024]{1,0:T(8,128)(2,1)S(1)}, bf16[128,1024]{1,0:T(8,128)(2,1)S(1)}, u32[]{:S(2)}, u32[]{:S(2)}) %collective-permute-start.1) | collective-permute-done | bytes 262176 | tf_op jit(solution)/shard_map/ppermute | solution.py:54
  33.5 1.6 %collective-permute-start.18 = (bf16[2,128,512]{2,1,0:T(8,128)(2,1)S(1)}, bf16[2,128,512]{2,1,0:T(8,128)(2,1)S(1)}, u32[]{:S(2)}, u32[]{:S(2)}) collective-permute-start(bf16[2,128,512]{2,1,0:T(8,128)(2,1)S(1)} %shard_map.81), channel_id=1, source_target_pairs={{0,2},{1,3},{2,0},{3,1},{4,6},{5,7},{6,4},{7,5},{8,10},{9,11},{10,... | collective-permute-start | bytes 786440 | tf_op jit(solution)/shard_map/ppermute | solution.py:54
  35.0 2.6 %collective-permute-done.2.refs_1_.refs_0_.refs_10_ = bf16[128,1024]{1,0:T(8,128)(2,1)S(1)} collective-permute-done((bf16[128,1024]{1,0:T(8,128)(2,1)S(1)}, bf16[128,1024]{1,0:T(8,128)(2,1)S(1)}, u32[]{:S(2)}, u32[]{:S(2)}) %collective-permute-start.2) | collective-permute-done | bytes 262176 | tf_op jit(solution)/shard_map/ppermute | solution.py:54
  39.2 2.5 %shard_map.79.refs_3_ = f32[256,768]{1,0:T(8,128)S(1)} custom-call(bf16[256,4096]{1,0:T(8,128)(2,1)S(1)} %get-tuple-element.16.refs_0_.refs_1_, bf16[128,1024]{1,0:T(8,128)(2,1)S(1)} %collective-permute-done.4.refs_0_.refs_1_.refs_4_, bf16[128,1024]{1,0:T(8,128)(2,1)S(1)} %collective-permute-done.5.refs_1_.refs_2_.refs_5_, ...), custom_call_target="tpu_custom_call" | custom-call | flops 1073741824 | bytes 8126464 | tf_op jit(solution)/shard_map/pallas_call | solution.py:262
  45.0 3.9 %collective-permute-done.22.refs_7_ = bf16[272,256]{1,0:T(8,128)(2,1)S(1)} collective-permute-done((bf16[272,256]{1,0:T(8,128)(2,1)S(1)}, bf16[272,256]{1,0:T(8,128)(2,1)S(1)}, u32[]{:S(2)}, u32[]{:S(2)}) %collective-permute-start.22) | collective-permute-done | bytes 139296 | tf_op jit(solution)/shard_map/ppermute | solution.py:54
  48.9 2.3 %collective-permute-done.19.refs_3_.refs_21_ = bf16[1,128,512]{2,1,0:T(8,128)(2,1)S(1)} collective-permute-done((bf16[1,128,512]{2,1,0:T(8,128)(2,1)S(1)}, bf16[1,128,512]{2,1,0:T(8,128)(2,1)S(1)}, u32[]{:S(2)}, u32[]{:S(2)}) %collective-permute-start.19) | collective-permute-done | bytes 131104 | tf_op jit(solution)/shard_map/ppermute | solution.py:54
  52.6 6.4 %shard_map.83 = (bf16[256,512]{1,0:T(8,128)(2,1)}, bf16[256,512]{1,0:T(8,128)(2,1)S(1)}, bf16[512,256]{1,0:T(8,128)(2,1)S(1)}, f32[512,256]{1,0:T(8,128)S(1)}) custom-call(f32[256,512]{1,0:T(8,128)S(1)} %get-tuple-element.18.refs_0_, bf16[256,4096]{1,0:T(8,128)(2,1)S(1)} %get-tuple-element.16.refs_0_.refs_1_, ...), custom_call_target="tpu_custom_call" | custom-call | flops 1879048192 | bytes 5799936 | tf_op jit(solution)/shard_map/pallas_call | solution.py:262
  61.9 4.3 %collective-permute-done.26.refs_2_ = bf16[256,256]{1,0:T(8,128)(2,1)S(1)} collective-permute-done((bf16[256,256]{1,0:T(8,128)(2,1)S(1)}, bf16[256,256]{1,0:T(8,128)(2,1)S(1)}, u32[]{:S(2)}, u32[]{:S(2)}) %collective-permute-start.26) | collective-permute-done | bytes 131104 | tf_op jit(solution)/shard_map/ppermute | solution.py:54
  74.8 1.6 %collective-permute-start.38 = (bf16[2,128,512]{2,1,0:T(8,128)(2,1)S(1)}, bf16[2,128,512]{2,1,0:T(8,128)(2,1)S(1)}, u32[]{:S(2)}, u32[]{:S(2)}) collective-permute-start(bf16[2,128,512]{2,1,0:T(8,128)(2,1)S(1)} %shard_map.98), channel_id=1, source_target_pairs={{0,2},{1,3},{2,0},{3,1},{4,6},{5,7},{6,4},{7,5},{8,10},{9,11},{10,... | collective-permute-start | bytes 786440 | tf_op jit(solution)/shard_map/ppermute | solution.py:54
  76.4 3.5 %collective-permute-done.32.refs_3_.refs_4_ = bf16[2,128,512]{2,1,0:T(8,128)(2,1)S(1)} collective-permute-done((bf16[2,128,512]{2,1,0:T(8,128)(2,1)S(1)}, bf16[2,128,512]{2,1,0:T(8,128)(2,1)S(1)}, u32[]{:S(2)}, u32[]{:S(2)}) %collective-permute-start.32) | collective-permute-done | bytes 262176 | tf_op jit(solution)/shard_map/ppermute | solution.py:54
  81.4 4.1 %collective-permute-done.33.refs_3_.refs_5_ = bf16[2,128,512]{2,1,0:T(8,128)(2,1)S(1)} collective-permute-done((bf16[2,128,512]{2,1,0:T(8,128)(2,1)S(1)}, bf16[2,128,512]{2,1,0:T(8,128)(2,1)S(1)}, u32[]{:S(2)}, u32[]{:S(2)}) %collective-permute-start.33) | collective-permute-done | bytes 262176 | tf_op jit(solution)/shard_map/ppermute | solution.py:54
  88.3 1.7 %collective-permute-start.44 = (bf16[256,512]{1,0:T(8,128)(2,1)S(1)}, bf16[256,512]{1,0:T(8,128)(2,1)S(1)}, u32[]{:S(2)}, u32[]{:S(2)}) collective-permute-start(bf16[256,512]{1,0:T(8,128)(2,1)S(1)} %shard_map.104), channel_id=1, source_target_pairs={{0,8},{4,12},{8,0},{12,4},{16,24},{20,28},{24,16},{28,20},{1,9},{5... | collective-permute-start | bytes 786440 | tf_op jit(solution)/shard_map/ppermute | solution.py:54
  92.4 1.7 %collective-permute-start.36 = (bf16[256,512]{1,0:T(8,128)(2,1)S(1)}, bf16[256,512]{1,0:T(8,128)(2,1)S(1)}, u32[]{:S(2)}, u32[]{:S(2)}) collective-permute-start(bf16[256,512]{1,0:T(8,128)(2,1)S(1)} %shard_map.96), channel_id=1, source_target_pairs={{0,8},{4,12},{8,0},{12,4},{16,24},{20,28},{24,16},{28,20},{1,9},{5... | collective-permute-start | bytes 786440 | tf_op jit(solution)/shard_map/ppermute | solution.py:54
  96.6 2.1 %collective-permute-done.44.refs_4_ = bf16[256,512]{1,0:T(8,128)(2,1)S(1)} collective-permute-done((bf16[256,512]{1,0:T(8,128)(2,1)S(1)}, bf16[256,512]{1,0:T(8,128)(2,1)S(1)}, u32[]{:S(2)}, u32[]{:S(2)}) %collective-permute-start.44) | collective-permute-done | bytes 262176 | tf_op jit(solution)/shard_map/ppermute | solution.py:54
  102.1 3.8 %collective-permute-start.40 = (bf16[128,512]{1,0:T(8,128)(2,1)S(1)}, bf16[128,512]{1,0:T(8,128)(2,1)S(1)}, u32[]{:S(2)}, u32[]{:S(2)}) collective-permute-start(bf16[128,512]{1,0:T(8,128)(2,1)S(1)} %shard_map.100), channel_id=1, source_target_pairs={{0,16},{4,20},{8,24},{12,28},{16,0},{20,4},{24,8},{28,12},{1,17},{... | collective-permute-start | bytes 393224 | tf_op jit(solution)/shard_map/ppermute | solution.py:54
  105.8 2.0 %collective-permute-done.45.refs_5_ = bf16[128,512]{1,0:T(8,128)(2,1)S(1)} collective-permute-done((bf16[128,512]{1,0:T(8,128)(2,1)S(1)}, bf16[128,512]{1,0:T(8,128)(2,1)S(1)}, u32[]{:S(2)}, u32[]{:S(2)}) %collective-permute-start.45) | collective-permute-done | bytes 131104 | tf_op jit(solution)/shard_map/ppermute | solution.py:54
  109.4 5.3 %shard_map.86 = bf16[256,4096]{1,0:T(8,128)(2,1)} custom-call(s32[2]{0:T(128)S(1)} %pad_add_fusion.refs_0_, bf16[256,512]{1,0:T(8,128)(2,1)S(1)} %get-tuple-element.21.refs_1_, bf16[256,256]{1,0:T(8,128)(2,1)S(1)} %shard_map.85.refs_2_.refs_1_, bf16[512,768]{1,0:T(8,128)(2,1)S(1)} %copy-done, ...), custom_call_target="tpu_custom_call" | custom-call | flops 1610612736 | bytes 8781824 | tf_op jit(solution)/shard_map/pallas_call | solution.py:262
  (126 shorter events, 42.8 us)
Async XLA Ops:
  2.6 13.7 %collective-permute-start.5 = (bf16[128,1024]{1,0:T(8,128)(2,1)S(1)}, bf16[128,1024]{1,0:T(8,128)(2,1)S(1)}, u32[]{:S(2)}, u32[]{:S(2)}) collective-permute-start(bf16[128,1024]{1,0:T(8,128)(2,1)S(1)} %pad_maximum_fusion), channel_id=1, source_target_pairs={{0,8},{4,12},{8,0},{12,4},{16,24},{20,28},{24,16},{28,20},{1,9},{5... | collective-permute-start | bytes 786440 | tf_op jit(solution)/shard_map/ppermute | solution.py:54
  5.8 14.0 %collective-permute-start.4 = (bf16[128,1024]{1,0:T(8,128)(2,1)S(1)}, bf16[128,1024]{1,0:T(8,128)(2,1)S(1)}, u32[]{:S(2)}, u32[]{:S(2)}) collective-permute-start(bf16[128,1024]{1,0:T(8,128)(2,1)S(1)} %pad_maximum_fusion), channel_id=1, source_target_pairs={{0,4},{4,0},{8,12},{12,8},{16,20},{20,16},{24,28},{28,24},{1,5},{5... | collective-permute-start | bytes 786440 | tf_op jit(solution)/shard_map/ppermute | solution.py:54
  7.3 14.6 %collective-permute-start = (bf16[128,1024]{1,0:T(8,128)(2,1)S(1)}, bf16[128,1024]{1,0:T(8,128)(2,1)S(1)}, u32[]{:S(2)}, u32[]{:S(2)}) collective-permute-start(bf16[128,1024]{1,0:T(8,128)(2,1)S(1)} %pad_maximum_fusion), channel_id=1, source_target_pairs={{0,16},{4,20},{8,24},{12,28},{16,0},{20,4},{24,8},{28,12},{1,17},{... | collective-permute-start | bytes 786440 | tf_op jit(solution)/shard_map/ppermute | solution.py:54
  16.3 8.1 %collective-permute-start.6 = (bf16[128,1024]{1,0:T(8,128)(2,1)S(1)}, bf16[128,1024]{1,0:T(8,128)(2,1)S(1)}, u32[]{:S(2)}, u32[]{:S(2)}) collective-permute-start(bf16[128,1024]{1,0:T(8,128)(2,1)S(1)} %collective-permute-done.5.refs_1_.refs_2_.refs_5_), channel_id=1, source_target_pairs={{0,4},{4,0},{8,12},{12,8},{16,20},{20,16},{24,28},{28,24},{1,5},{5... | collective-permute-start | bytes 786440 | tf_op jit(solution)/shard_map/ppermute | solution.py:54
  19.8 7.0 %collective-permute-start.8 = (bf16[2,128,512]{2,1,0:T(8,128)(2,1)S(1)}, bf16[2,128,512]{2,1,0:T(8,128)(2,1)S(1)}, u32[]{:S(2)}, u32[]{:S(2)}) collective-permute-start(bf16[2,128,512]{2,1,0:T(8,128)(2,1)S(1)} %shard_map.77), channel_id=1, source_target_pairs={{0,2},{1,3},{2,0},{3,1},{4,6},{5,7},{6,4},{7,5},{8,10},{9,11},{10,... | collective-permute-start | bytes 786440 | tf_op jit(solution)/shard_map/ppermute | solution.py:54
  24.5 8.2 %collective-permute-start.7 = (bf16[128,1024]{1,0:T(8,128)(2,1)S(1)}, bf16[128,1024]{1,0:T(8,128)(2,1)S(1)}, u32[]{:S(2)}, u32[]{:S(2)}) collective-permute-start(bf16[128,1024]{1,0:T(8,128)(2,1)S(1)} %collective-permute-done.refs_1_.refs_4_.refs_7_), channel_id=1, source_target_pairs={{0,4},{4,0},{8,12},{12,8},{16,20},{20,16},{24,28},{28,24},{1,5},{5... | collective-permute-start | bytes 786440 | tf_op jit(solution)/shard_map/ppermute | solution.py:54
  33.5 11.0 %collective-permute-start.18 = (bf16[2,128,512]{2,1,0:T(8,128)(2,1)S(1)}, bf16[2,128,512]{2,1,0:T(8,128)(2,1)S(1)}, u32[]{:S(2)}, u32[]{:S(2)}) collective-permute-start(bf16[2,128,512]{2,1,0:T(8,128)(2,1)S(1)} %shard_map.81), channel_id=1, source_target_pairs={{0,2},{1,3},{2,0},{3,1},{4,6},{5,7},{6,4},{7,5},{8,10},{9,11},{10,... | collective-permute-start | bytes 786440 | tf_op jit(solution)/shard_map/ppermute | solution.py:54
  43.6 7.6 %collective-permute-start.19 = (bf16[1,128,512]{2,1,0:T(8,128)(2,1)S(1)}, bf16[1,128,512]{2,1,0:T(8,128)(2,1)S(1)}, u32[]{:S(2)}, u32[]{:S(2)}) collective-permute-start(bf16[1,128,512]{2,1,0:T(8,128)(2,1)S(1)} %shard_map.82), channel_id=1, source_target_pairs={{0,2},{1,3},{2,0},{3,1},{4,6},{5,7},{6,4},{7,5},{8,10},{9,11},{10,... | collective-permute-start | bytes 393224 | tf_op jit(solution)/shard_map/ppermute | solution.py:54
  44.5 8.1 %collective-permute-start.20 = (bf16[2,128,512]{2,1,0:T(8,128)(2,1)S(1)}, bf16[2,128,512]{2,1,0:T(8,128)(2,1)S(1)}, u32[]{:S(2)}, u32[]{:S(2)}) collective-permute-start(bf16[2,128,512]{2,1,0:T(8,128)(2,1)S(1)} %collective-permute-done.18.refs_2_.refs_20_), channel_id=1, source_target_pairs={{0,1},{1,0},{2,3},{3,2},{4,5},{5,4},{6,7},{7,6},{8,9},{9,8},{10,11... | collective-permute-start | bytes 786440 | tf_op jit(solution)/shard_map/ppermute | solution.py:54
  44.5 8.1 %collective-permute-start.23 = (bf16[272,256]{1,0:T(8,128)(2,1)S(1)}, bf16[272,256]{1,0:T(8,128)(2,1)S(1)}, u32[]{:S(2)}, u32[]{:S(2)}) collective-permute-start(bf16[272,256]{1,0:T(8,128)(2,1)S(1)} %get-tuple-element.19.refs_6_), channel_id=1, source_target_pairs={{0,1},{1,0},{2,3},{3,2},{4,5},{5,4},{6,7},{7,6},{8,9},{9,8},{10,11... | collective-permute-start | bytes 417800 | tf_op jit(solution)/shard_map/ppermute | solution.py:54
  69.4 18.9 %collective-permute-start.27 = (bf16[512,512]{1,0:T(8,128)(2,1)S(1)}, bf16[512,512]{1,0:T(8,128)(2,1)S(1)}, u32[]{:S(2)}, u32[]{:S(2)}) collective-permute-start(bf16[512,512]{1,0:T(8,128)(2,1)S(1)} %shard_map.87), channel_id=1, source_target_pairs={{0,1},{1,0},{2,3},{3,2},{4,5},{5,4},{6,7},{7,6},{8,9},{9,8},{10,11... | collective-permute-start | bytes 1572872 | tf_op jit(solution)/shard_map/ppermute | solution.py:54
  70.6 9.2 %collective-permute-start.32 = (bf16[2,128,512]{2,1,0:T(8,128)(2,1)S(1)}, bf16[2,128,512]{2,1,0:T(8,128)(2,1)S(1)}, u32[]{:S(2)}, u32[]{:S(2)}) collective-permute-start(bf16[2,128,512]{2,1,0:T(8,128)(2,1)S(1)} %shard_map.92), channel_id=1, source_target_pairs={{0,2},{1,3},{2,0},{3,1},{4,6},{5,7},{6,4},{7,5},{8,10},{9,11},{10,... | collective-permute-start | bytes 786440 | tf_op jit(solution)/shard_map/ppermute | solution.py:54
  72.2 13.3 %collective-permute-start.33 = (bf16[2,128,512]{2,1,0:T(8,128)(2,1)S(1)}, bf16[2,128,512]{2,1,0:T(8,128)(2,1)S(1)}, u32[]{:S(2)}, u32[]{:S(2)}) collective-permute-start(bf16[2,128,512]{2,1,0:T(8,128)(2,1)S(1)} %shard_map.93), channel_id=1, source_target_pairs={{0,2},{1,3},{2,0},{3,1},{4,6},{5,7},{6,4},{7,5},{8,10},{9,11},{10,... | collective-permute-start | bytes 786440 | tf_op jit(solution)/shard_map/ppermute | solution.py:54
  73.3 14.0 %collective-permute-start.43 = (bf16[256,512]{1,0:T(8,128)(2,1)S(1)}, bf16[256,512]{1,0:T(8,128)(2,1)S(1)}, u32[]{:S(2)}, u32[]{:S(2)}) collective-permute-start(bf16[256,512]{1,0:T(8,128)(2,1)S(1)} %shard_map.103), channel_id=1, source_target_pairs={{0,4},{4,0},{8,12},{12,8},{16,20},{20,16},{24,28},{28,24},{1,5},{5... | collective-permute-start | bytes 786440 | tf_op jit(solution)/shard_map/ppermute | solution.py:54
  74.8 19.2 %collective-permute-start.38 = (bf16[2,128,512]{2,1,0:T(8,128)(2,1)S(1)}, bf16[2,128,512]{2,1,0:T(8,128)(2,1)S(1)}, u32[]{:S(2)}, u32[]{:S(2)}) collective-permute-start(bf16[2,128,512]{2,1,0:T(8,128)(2,1)S(1)} %shard_map.98), channel_id=1, source_target_pairs={{0,2},{1,3},{2,0},{3,1},{4,6},{5,7},{6,4},{7,5},{8,10},{9,11},{10,... | collective-permute-start | bytes 786440 | tf_op jit(solution)/shard_map/ppermute | solution.py:54
  80.1 10.2 %collective-permute-start.34 = (bf16[128,512]{1,0:T(8,128)(2,1)S(1)}, bf16[128,512]{1,0:T(8,128)(2,1)S(1)}, u32[]{:S(2)}, u32[]{:S(2)}) collective-permute-start(bf16[128,512]{1,0:T(8,128)(2,1)S(1)} %shard_map.94), channel_id=1, source_target_pairs={{0,4},{4,0},{8,12},{12,8},{16,20},{20,16},{24,28},{28,24},{1,5},{5... | collective-permute-start | bytes 393224 | tf_op jit(solution)/shard_map/ppermute | solution.py:54
  87.3 9.3 %collective-permute-start.42 = (bf16[256,512]{1,0:T(8,128)(2,1)S(1)}, bf16[256,512]{1,0:T(8,128)(2,1)S(1)}, u32[]{:S(2)}, u32[]{:S(2)}) collective-permute-start(bf16[256,512]{1,0:T(8,128)(2,1)S(1)} %shard_map.102), channel_id=1, source_target_pairs={{0,4},{4,0},{8,12},{12,8},{16,20},{20,16},{24,28},{28,24},{1,5},{5... | collective-permute-start | bytes 786440 | tf_op jit(solution)/shard_map/ppermute | solution.py:54
  88.3 10.4 %collective-permute-start.44 = (bf16[256,512]{1,0:T(8,128)(2,1)S(1)}, bf16[256,512]{1,0:T(8,128)(2,1)S(1)}, u32[]{:S(2)}, u32[]{:S(2)}) collective-permute-start(bf16[256,512]{1,0:T(8,128)(2,1)S(1)} %shard_map.104), channel_id=1, source_target_pairs={{0,8},{4,12},{8,0},{12,4},{16,24},{20,28},{24,16},{28,20},{1,9},{5... | collective-permute-start | bytes 786440 | tf_op jit(solution)/shard_map/ppermute | solution.py:54
  90.3 10.2 %collective-permute-start.28 = (bf16[2,128,512]{2,1,0:T(8,128)(2,1)S(1)}, bf16[2,128,512]{2,1,0:T(8,128)(2,1)S(1)}, u32[]{:S(2)}, u32[]{:S(2)}) collective-permute-start(bf16[2,128,512]{2,1,0:T(8,128)(2,1)S(1)} %shard_map.88), channel_id=1, source_target_pairs={{0,2},{1,3},{2,0},{3,1},{4,6},{5,7},{6,4},{7,5},{8,10},{9,11},{10,... | collective-permute-start | bytes 786440 | tf_op jit(solution)/shard_map/ppermute | solution.py:54
  92.4 9.4 %collective-permute-start.36 = (bf16[256,512]{1,0:T(8,128)(2,1)S(1)}, bf16[256,512]{1,0:T(8,128)(2,1)S(1)}, u32[]{:S(2)}, u32[]{:S(2)}) collective-permute-start(bf16[256,512]{1,0:T(8,128)(2,1)S(1)} %shard_map.96), channel_id=1, source_target_pairs={{0,8},{4,12},{8,0},{12,4},{16,24},{20,28},{24,16},{28,20},{1,9},{5... | collective-permute-start | bytes 786440 | tf_op jit(solution)/shard_map/ppermute | solution.py:54
  94.3 7.6 %collective-permute-start.39 = (bf16[128,512]{1,0:T(8,128)(2,1)S(1)}, bf16[128,512]{1,0:T(8,128)(2,1)S(1)}, u32[]{:S(2)}, u32[]{:S(2)}) collective-permute-start(bf16[128,512]{1,0:T(8,128)(2,1)S(1)} %shard_map.99), channel_id=1, source_target_pairs={{0,4},{4,0},{8,12},{12,8},{16,20},{20,16},{24,28},{28,24},{1,5},{5... | collective-permute-start | bytes 393224 | tf_op jit(solution)/shard_map/ppermute | solution.py:54
  98.9 8.9 %collective-permute-start.45 = (bf16[128,512]{1,0:T(8,128)(2,1)S(1)}, bf16[128,512]{1,0:T(8,128)(2,1)S(1)}, u32[]{:S(2)}, u32[]{:S(2)}) collective-permute-start(bf16[128,512]{1,0:T(8,128)(2,1)S(1)} %shard_map.105), channel_id=1, source_target_pairs={{0,16},{4,20},{8,24},{12,28},{16,0},{20,4},{24,8},{28,12},{1,17},{... | collective-permute-start | bytes 393224 | tf_op jit(solution)/shard_map/ppermute | solution.py:54
  100.7 14.0 %collective-permute-start.29 = (bf16[128,512]{1,0:T(8,128)(2,1)S(1)}, bf16[128,512]{1,0:T(8,128)(2,1)S(1)}, u32[]{:S(2)}, u32[]{:S(2)}) collective-permute-start(bf16[128,512]{1,0:T(8,128)(2,1)S(1)} %shard_map.89), channel_id=1, source_target_pairs={{0,4},{4,0},{8,12},{12,8},{16,20},{20,16},{24,28},{28,24},{1,5},{5... | collective-permute-start | bytes 393224 | tf_op jit(solution)/shard_map/ppermute | solution.py:54
  102.1 12.6 %collective-permute-start.40 = (bf16[128,512]{1,0:T(8,128)(2,1)S(1)}, bf16[128,512]{1,0:T(8,128)(2,1)S(1)}, u32[]{:S(2)}, u32[]{:S(2)}) collective-permute-start(bf16[128,512]{1,0:T(8,128)(2,1)S(1)} %shard_map.100), channel_id=1, source_target_pairs={{0,16},{4,20},{8,24},{12,28},{16,0},{20,4},{24,8},{28,12},{1,17},{... | collective-permute-start | bytes 393224 | tf_op jit(solution)/shard_map/ppermute | solution.py:54
  (27 other events, 214.4 us)
